TPU v7x, 512 devices: a whole 4x8x8 slice. The times are simulated.
512 devices in a mesh: seq: 16 (over x_hi, z), head: 32 (over y, x_lo, core).
Axes of the slice: x: 4 (x_hi: 2, x_lo: 2; x = x_hi * 2 + x_lo), y: 8, z: 8, core: 2. Of those that a mesh axis runs over, the one named last changes fastest.
Arguments:
- query: bfloat16 [160, 2048, 128], P('head', 'seq'), may hold values from -1024 to 1024
- key: bfloat16 [160, 2048, 128], P('head', 'seq'), may hold values from -1024 to 1024
- value: bfloat16 [160, 2048, 128], P('head', 'seq'), may hold values from -6 to 6
- q_gain: float32 [40, 128], replicated, may hold values from 0.8 to 2
- k_gain: float32 [40, 128], replicated, may hold values from 0.8 to 2
- order: int32 [160, 2048], P('head', 'seq'), may hold values from 0 to 2047, as said below
- cluster_rows: int32 [160, 16], P('head'), may hold values from 0 to 256, as said below
- block_map: int32 [160, 32, 32], P('head'), may hold values 0 or 1
Outputs:
- attended: bfloat16 [160, 2048, 128], P('head', 'seq')
Inputs may be any that keep to these rules, and one draw needn't show every extreme that they name: `order`: each stream's row lists every token row once: the rows of cluster 0 first, then those of cluster 1, and so on, in the counts of cluster_rows. `cluster_rows`: each stream's counts sum to 2048; of the 128 token rows of one seq index at most 16 belong to one cluster, and in every stream one cluster takes exactly 16 rows from every seq index.
All inputs are finite; a program needn't handle non-finite values. No bound on the sum of `block_map` on one device may be relied on, other than what follows from the above.
Results may differ from a plain program's by a relative error of at most 0.012.
The roundings to bfloat16 on the way count: a program that leaves them out, or rounds other values in their place, can miss the bound.
Values may be sent and summed in bfloat16 or wider, within the bound.
A program may use at most 64 MiB of HBM per device.

v0:
```python
import jax
import jax.numpy as jnp
from jax import lax
from jax.sharding import Mesh
from jax.sharding import PartitionSpec as P

BLOCK = 128
SEQ = ("seq_0", "seq_1")


epsilon = 1e-06
floor_score = -1e30
key_block = 256


def from_everyone(x, axis):
    size = lax.axis_size(axis)
    return lax.all_to_all(jnp.broadcast_to(x[None], (size, *x.shape)), axis, 0, 0, tiled=True)


def taken_together(x, axis):
    return from_everyone(x, axis).sum(axis=0)


def packed_total(arrays, axis):
    flat, at, gathered = (jnp.concatenate([a.reshape(-1) for a in arrays]), 0, [])
    subtotal = taken_together(flat, axis)
    for a in arrays:
        gathered.append(subtotal[at : at + a.size].reshape(a.shape))
        at += a.size
    return tuple(gathered)


def in_order(blocks, dim):
    blocks = jnp.moveaxis(blocks, 0, dim)
    shape = blocks.shape
    return blocks.reshape(*shape[:dim], shape[dim] * shape[dim + 1], *shape[dim + 2 :])


def gather_in_order(x, axes, order):
    blocks = x
    for k in order:
        blocks = lax.all_gather(blocks, axes[k])
    done = order[::-1]
    back = [done.index(k) for k in range(len(axes))]
    blocks = blocks.transpose(*back, *range(len(axes), blocks.ndim))
    return blocks.reshape(-1, *x.shape)


def gathered_by_axis(x, axes, order, dim):
    return in_order(gather_in_order(x, axes, order), dim)


def sent_together(arrays, axis, dim, along):
    ends, at = ([], 0)
    for a in arrays[:-1]:
        at += a.shape[along]
        ends.append(at)
    both = jnp.concatenate(arrays, axis=along)
    return tuple(jnp.split(lax.all_gather(both, axis, axis=dim, tiled=True), ends, axis=along))


def absorb(running, scores, allowed, value_rows):
    row_peak, denom_sum, numerator = running
    masked = jnp.where(allowed, scores, floor_score)
    new_peak = jnp.maximum(row_peak, jnp.max(masked, axis=2))
    weights = jnp.where(allowed, jnp.exp(masked - new_peak[:, :, None]), 0.0)
    rescale = jnp.exp(row_peak - new_peak)
    denom_sum = denom_sum * rescale + jnp.sum(weights, axis=2)
    numerator = numerator * rescale[:, :, None] + jnp.einsum(
        "sqk,skd->sqd", weights.astype(jnp.bfloat16), value_rows, preferred_element_type=jnp.float32
    )
    return (new_peak, denom_sum, numerator)


def fold_keys(running, key_rows, value_rows, score_fn):
    row_count = key_rows.shape[1]

    def visit_block(block_index, inner_state):
        first_row = block_index * key_block
        key_part = lax.dynamic_slice_in_dim(key_rows, first_row, key_block, 1)
        value_part = lax.dynamic_slice_in_dim(value_rows, first_row, key_block, 1)
        return score_fn(inner_state, key_part, value_part, first_row)

    return lax.fori_loop(0, row_count // key_block, visit_block, running)


def normalize(rows, gain_rows, scale_rows):
    return (rows.astype(jnp.float32) * scale_rows[None, :, None] * gain_rows[:, None, :]).astype(
        jnp.bfloat16
    )


def local(query, key, value, q_gain, k_gain, order, cluster_rows, block_map):
    streams, tok_rows, head_width = query.shape
    head_count = q_gain.shape[0]
    seq_count = lax.axis_size(SEQ)
    seq_rank = lax.axis_index(SEQ)
    head_rank = lax.axis_index("head")
    videos = streams * lax.axis_size("head") // head_count
    first_stream = head_rank * streams
    video_pick = (jnp.arange(videos) == first_stream // head_count).astype(jnp.float32)
    square_q = jnp.sum(jnp.square(query.astype(jnp.float32)), axis=(0, 2))
    square_k = jnp.sum(jnp.square(key.astype(jnp.float32)), axis=(0, 2))
    totals = packed_total((square_q[:, None] * video_pick, square_k[:, None] * video_pick), "head")
    norm_width = head_count * head_width
    scale_q = lax.rsqrt(jnp.sum(totals[0] * video_pick, axis=1) / norm_width + epsilon)
    scale_k = lax.rsqrt(jnp.sum(totals[1] * video_pick, axis=1) / norm_width + epsilon)
    first_head = first_stream % head_count
    normed_q = normalize(query, lax.dynamic_slice_in_dim(q_gain, first_head, streams, 0), scale_q)
    normed_k = normalize(key, lax.dynamic_slice_in_dim(k_gain, first_head, streams, 0), scale_k)
    full_order = gathered_by_axis(order, SEQ, (0, 1), 1)
    seq_length = full_order.shape[1]
    positions = jnp.arange(seq_length, dtype=jnp.int32)
    stream_index = jnp.arange(streams, dtype=jnp.int32)[:, None]
    inverse = (
        jnp.zeros((streams, seq_length), jnp.int32)
        .at[stream_index, full_order]
        .set(jnp.broadcast_to(positions, (streams, seq_length)))
    )
    cluster_start = jnp.cumsum(cluster_rows, axis=1, dtype=jnp.int32) - cluster_rows
    cluster_axis = jnp.arange(seq_count, dtype=jnp.int32)
    owner_index = (
        jnp.sum(
            (cluster_start[:, None, :] <= inverse[:, :, None]).astype(jnp.int32),
            axis=2,
            dtype=jnp.int32,
        )
        - 1
    )
    owner_hit = owner_index[:, :, None] == cluster_axis
    owner_start = jnp.sum(
        jnp.where(owner_hit, cluster_start[:, None, :], 0), axis=2, dtype=jnp.int32
    )
    capacity = 2 * tok_rows
    blocks_per = capacity // BLOCK
    token_block = owner_index * blocks_per + (inverse - owner_start) // BLOCK
    block_count = block_map.shape[2]
    block_axis = jnp.arange(block_count, dtype=jnp.int32)
    score_scale = head_width ** (-0.5)
    my_tokens = seq_rank * tok_rows
    my_block = lax.dynamic_slice_in_dim(token_block, my_tokens, tok_rows, 1)
    row_table = jnp.einsum(
        "stn,snm->stm",
        (my_block[:, :, None] == block_axis).astype(jnp.float32),
        block_map.astype(jnp.float32),
    )

    def score_tokens(inner_state, key_part, value_part, offset):
        key_span = key_part.shape[1]
        key_ids = lax.dynamic_slice_in_dim(token_block, offset, key_span, 1)
        allowed = (
            jnp.einsum(
                "stm,skm->stk", row_table, (key_ids[:, :, None] == block_axis).astype(jnp.float32)
            )
            > 0.5
        )
        allowed = allowed | (my_block[:, :, None] == key_ids[:, None, :])
        scores = (
            jnp.einsum("sqd,skd->sqk", normed_q, key_part, preferred_element_type=jnp.float32)
            * score_scale
        )
        return absorb(inner_state, scores, allowed, value_part)

    start_state = (
        jnp.full((streams, tok_rows), floor_score, jnp.float32),
        jnp.zeros((streams, tok_rows), jnp.float32),
        jnp.zeros((streams, tok_rows, head_width), jnp.float32),
    )
    kv_piece = sent_together((normed_k, value), SEQ, 1, 0)
    row_peak, denom_sum, numerator = fold_keys(start_state, kv_piece[0], kv_piece[1], score_tokens)
    result = (numerator / denom_sum[:, :, None]).astype(jnp.bfloat16)
    return result


def solution(mesh):
    finer = Mesh(mesh.devices.reshape(2, 8, mesh.shape["head"]), ("seq_0", "seq_1", "head"))
    return jax.shard_map(
        local,
        mesh=finer,
        in_specs=(
            P("head", SEQ, None),
            P("head", SEQ, None),
            P("head", SEQ, None),
            P(),
            P(),
            P("head", SEQ),
            P("head", None),
            P("head", None, None),
        ),
        out_specs=P("head", SEQ, None),
        check_vma=False,
    )
```

profile of v0, /device:TPU:1, one launch (start us, length us, event | category | flops | bytes accessed | tf_op | source)
XLA Modules:
  0.0 180.6 jit_solution(16860229407675532183)
XLA Ops:
  6.6 1.2 fusion.18
  8.2 0.7 broadcast_in_dim.92
  8.9 10.4 %all-to-all-start = ((f32[32,1,1024]{2,1,0:T(1,128)}), f32[32,1,1024]{2,1,0:T(1,128)S(1)}, u32[]{:S(2)}, u32[]{:S(2)}) async-start(f32[32,1,1024]{2,1,0:T(1,128)} %broadcast_in_dim.92), calls=%async_computation | async-start | bytes 262144 | tf_op jit(solution)/shard_map/all_to_all | solution.py:18
  19.3 9.3 %all-to-all-done = f32[32,1,1024]{2,1,0:T(1,128)S(1)} async-done(((f32[32,1,1024]{2,1,0:T(1,128)}), f32[32,1,1024]{2,1,0:T(1,128)S(1)}, u32[]{:S(2)}, u32[]{:S(2)}) %all-to-all-start) | async-done | bytes 131104 | tf_op jit(solution)/shard_map/all_to_all | solution.py:18
  29.1 1.0 fusion.20
  30.2 1.7 pad_maximum_fusion
  31.9 4.7 %all-gather.2 = s32[2,5,128]{2,1,0:T(8,128)S(1)} all-gather(s32[1,5,128]{2,1,0:T(8,128)S(1)} %bitcast.27), channel_id=2, replica_groups=mesh['seq_0'=2,'seq_1'=8,'head'=32] {'seq_0'}, dimensions={0}, use_global_device_ids=true | all-gather | bytes 7680 | tf_op jit(solution)/shard_map/all_gather | solution.py:43
  36.6 24.9 %all-gather.1 = s32[16,5,128]{2,1,0:T(8,128)S(1)} all-gather(s32[2,5,128]{2,1,0:T(8,128)S(1)} %all-gather.2), channel_id=3, replica_groups=mesh['seq_0'=2,'seq_1'=8,'head'=32] {'seq_1'}, dimensions={0}, use_global_device_ids=true | all-gather | bytes 46080 | tf_op jit(solution)/shard_map/all_gather | solution.py:43
  61.9 37.9 %scatter_custom_fusion = s32[10240]{0:T(1024)S(1)} fusion(s32[10240]{0:T(1024)S(1)} %reshape.106, s32[10240]{0:T(1024)S(1)} %reshape.108, s32[]{:T(128)} %constant.116.clone.1), kind=kCustom, calls=%fused_computation.65 | custom fusion | bytes 40964
  99.8 0.2 reduce_window_sum.11
  100.0 0.7 constant_dynamic-slice_fusion.1
  100.7 0.2 convert_reduce_fusion
  100.9 0.2 select_reduce_fusion
  101.2 0.2 fusion.24
  101.6 39.2 %all-gather.5.cloned.1.call-done = bf16[10,2048,128]{2,1,0:T(8,128)(2,1)} async-done(((bf16[10,128,128]{2,1,0:T(8,128)(2,1)}), bf16[10,2048,128]{2,1,0:T(8,128)(2,1)}) %all-gather.5.cloned.1.call-update) | async-done | bytes 5242896 | tf_op jit(solution)/shard_map/all_gather | solution.py:60
  140.8 5.3 %fusion.33 = (bf16[5,2048,128]{2,1,0:T(8,128)(2,1)}, bf16[5,2048,128]{2,1,0:T(8,128)(2,1)}) fusion(bf16[10,2048,128]{2,1,0:T(8,128)(2,1)} %all-gather.5.cloned.1.call-done), kind=kLoop, calls=%fused_computation.75 | loop fusion | bytes 10485760 | tf_op jit(solution)/shard_map/split | solution.py:60
  146.1 26.8 %while.18 = (s32[]{:T(128)}, f32[5,128]{1,0:T(8,128)S(1)}, f32[5,128]{1,0:T(8,128)S(1)}, f32[5,128,128]{2,1,0:T(8,128)S(1)}, s32[5,2048]{1,0:T(8,128)S(1)}, /*in...) while((s32[]{:T(128)}, f32[5,128]{1,0:T(8,128)S(1)}, ...), condition=%wide.region_12.13_spmd.clone, body=%wide.region_9.12_spmd.clone.sunk | while | flops 96627840 | bytes 4196043 | solution.py:85
  146.1 0.4 fusion.49
  146.5 1.3 fusion.50
  147.8 0.2 fusion.51
  148.0 1.4 convolution_add_fusion.2
  149.5 0.4 fusion.49
  149.9 1.3 fusion.50
  151.2 0.2 fusion.51
  151.4 1.4 convolution_add_fusion.2
  152.8 0.4 fusion.49
  153.3 1.3 fusion.50
  154.6 0.2 fusion.51
  154.7 1.4 convolution_add_fusion.2
  156.2 0.4 fusion.49
  156.6 1.3 fusion.50
  157.9 0.2 fusion.51
  158.1 1.4 convolution_add_fusion.2
  159.5 0.4 fusion.49
  160.0 1.3 fusion.50
  161.3 0.2 fusion.51
  161.5 1.4 convolution_add_fusion.2
  162.9 0.4 fusion.49
  163.3 1.3 fusion.50
  164.6 0.2 fusion.51
  164.8 1.4 convolution_add_fusion.2
  166.3 0.4 fusion.49
  166.7 1.3 fusion.50
  168.2 1.4 convolution_add_fusion.2
  169.6 0.4 fusion.49
  170.1 1.3 fusion.50
  171.5 1.4 convolution_add_fusion.2
  173.0 0.8 divide_convert_fusion
  (83 shorter events, 1.9 us)
Async XLA Ops:
  6.5 12.8 %copy-start = (f32[40,128]{1,0:T(8,128)S(1)}, f32[40,128]{1,0:T(8,128)}, u32[]{:S(2)}) copy-start(f32[40,128]{1,0:T(8,128)} %param.14) | copy-start | bytes 61444
  6.5 55.0 %copy-start.6 = (s32[2]{0:T(128)S(1)}, s32[2]{0:T(128)}, u32[]{:S(2)}) copy-start(s32[2]{0:T(128)} %constant.142) | copy-start | bytes 28
  6.5 55.1 %copy-start.5 = (s32[2]{0:T(128)S(1)}, s32[2]{0:T(128)}, u32[]{:S(2)}) copy-start(s32[2]{0:T(128)} %constant.145) | copy-start | bytes 28
  6.5 94.9 %copy-start.1 = (bf16[5,128,128]{2,1,0:T(8,128)(2,1)S(1)}, bf16[5,128,128]{2,1,0:T(8,128)(2,1)}, u32[]{:S(2)}) copy-start(bf16[5,128,128]{2,1,0:T(8,128)(2,1)} %param.10) | copy-start | bytes 491524
  6.5 25.4 %copy-start.4 = (s32[5,128]{1,0:T(8,128)S(1)}, s32[5,128]{1,0:T(8,128)}, u32[]{:S(2)}) copy-start(s32[5,128]{1,0:T(8,128)} %param.15) | copy-start | bytes 7684
  6.5 93.3 %copy-start.3 = (s32[5,16]{1,0:T(8,128)S(1)}, s32[5,16]{1,0:T(8,128)}, u32[]{:S(2)}) copy-start(s32[5,16]{1,0:T(8,128)} %param.16) | copy-start | bytes 964
  6.6 94.7 %copy-start.2 = (s32[5,32,32]{2,1,0:T(8,128)S(1)}, s32[5,32,32]{2,1,0:T(8,128)}, u32[]{:S(2)}) copy-start(s32[5,32,32]{2,1,0:T(8,128)} %param.17) | copy-start | bytes 61444
  8.9 19.8 %all-to-all-start = ((f32[32,1,1024]{2,1,0:T(1,128)}), f32[32,1,1024]{2,1,0:T(1,128)S(1)}, u32[]{:S(2)}, u32[]{:S(2)}) async-start(f32[32,1,1024]{2,1,0:T(1,128)} %broadcast_in_dim.92), calls=%async_computation | async-start | bytes 262144 | tf_op jit(solution)/shard_map/all_to_all | solution.py:18
  19.2 121.6 %all-gather.5.cloned.1.call-start = ((), (), s32[]{:S(2)}) async-start(), calls=%async_computation.1 | async-start | bytes 5570560 | tf_op jit(solution)/shard_map/all_gather | solution.py:60
Sparse Core Ops, SparseCore 0:
  32.0 108.7 all-gather.4
where the time goes:
time: 184 us; the launch traced here: 181 us
  waiting for transfers between devices  48.6 us (26%)
  local copies, waits for them, and re-layouts  45.3 us (25%)
  blocking collectives  29.6 us (16%)
  matrix products  24.9 us (14%)
  between operations  13.8 us (8%)
  starting transfers between devices  10.4 us (6%)
  other arithmetic  7.47 us (4%)
    all_gather x1, waiting for transfers between devices, sent_together(): lax.all_gather(both, axis, axis=dim, tiled=True)  39.2 us
    unnamed x16, local copies, waits for them, and re-layouts  38 us
    all_gather x2, blocking collectives, gather_in_order(): blocks = lax.all_gather(blocks, axes[k])  29.6 us
    dot_general x8, matrix products, absorb(): jnp.einsum('sqk,skd->sqd', weights.astype(jnp.bfloat16), value_rows, pref...  11.1 us
    all_to_all x1, starting transfers between devices, from_everyone(): lax.all_to_all(jnp.broadcast_to(x[None], (size, *x.shape)), axis, 0, 0, t...  10.4 us
    dot_general x8, matrix products, score_tokens(): jnp.einsum('sqd,skd->sqk', normed_q, key_part, preferred_element_type=jnp...  10.2 us
    all_to_all x1, waiting for transfers between devices, from_everyone(): lax.all_to_all(jnp.broadcast_to(x[None], (size, *x.shape)), axis, 0, 0, t...  9.34 us
    split x1, local copies, waits for them, and re-layouts, sent_together(): jnp.split(lax.all_gather(both, axis, axis=dim, tiled=True), ends, axis=al...  5.28 us
  transfers between devices with their start and end apart: 2, of which 2 were waited for; matrix products, arithmetic and copies ran while one was open for 22% of the time, Pallas kernels for 0%

commit v1 on v0

v1 whole, which is shorter than its diff:
```python
import math

import jax
import jax.numpy as jnp
from jax import lax
from jax.experimental import pallas as pl
from jax.experimental.pallas import tpu as pltpu
from jax.sharding import PartitionSpec as P

MESH = pl.DeviceIdType.MESH
F32 = jnp.float32
BF16 = jnp.bfloat16

EPS = 1e-06
ROWS = 128
Z = 8
STREAMS = 5
HEADS = 40
GROUP = 8
CLUSTERS = 16
BLOCKS = 32
MASKED = -(2.0**30)
NEAR_FIRST = (0, 1, 7, 2, 6, 3, 5, 4)
FAR_FIRST = (4, 3, 5, 2, 6, 1, 7, 0)
KEY_CHUNK = 512


def owner_of(z, shift, core):
    v = lax.rem(z - shift + 3 * core + 16, Z)
    stream = jnp.minimum(v - 3 * core * (v // 7), STREAMS - 1)
    busy = jnp.logical_or(v < STREAMS - core, core * v == 7)
    return stream, busy


def kernel(
    q_hbm, k_hbm, v_hbm, qg_ref, kg_ref, order_ref, rows_ref, map_ref, out_ref,
    qraw, kraw, qn, kn, sum_out, sum_in, ord_out, ord_in, kbuf, vbuf, qbuf, obuf,
    oht, mbuf, s_scr, bt_scr, a_scr,
    raw_sem, sum_send, sum_recv, ord_send, ord_recv, kv_send, kv_recv, fwd_send, fwd_recv,
    ofw_send, ofw_recv, out_send, out_recv,
):
    me = lax.axis_index("seq")
    head = lax.axis_index("head")
    half, z = me // Z, lax.rem(me, Z)
    shift = 2 * lax.rem(head // 2, 2)
    core = lax.rem(head, 2)
    member = lax.rem(head, GROUP)
    video = head - member
    mine, busy = owner_of(z, shift, core)
    partner = {"seq": (1 - half) * Z + z}

    def column(d):
        return lax.rem(z + d, Z)

    barrier = pltpu.get_barrier_semaphore()
    for d in range(1, Z):
        pl.semaphore_signal(
            barrier, inc=1, device_id={"seq": half * Z + column(d)}, device_id_type=MESH
        )
        pl.semaphore_signal(
            barrier,
            inc=1,
            device_id={"head": video + lax.rem(member + d, GROUP)},
            device_id_type=MESH,
        )
    pl.semaphore_signal(barrier, inc=1, device_id=partner, device_id_type=MESH)

    q_in = pltpu.make_async_copy(q_hbm, qraw, raw_sem.at[0])
    k_in = pltpu.make_async_copy(k_hbm, kraw, raw_sem.at[1])
    q_in.start()
    k_in.start()
    sum_out[...] = jnp.zeros((8, ROWS), F32)
    for j in range(STREAMS):
        ord_out[j] = jnp.broadcast_to(order_ref[pl.ds(j, 1), :], (8, ROWS))

    def squares(raw):
        total = jnp.zeros((ROWS, ROWS), F32)
        for j in range(STREAMS):
            x = raw[j].astype(F32)
            total = total + x * x
        return jnp.sum(total.T, axis=0, keepdims=True)

    q_in.wait()
    sum_out[pl.ds(0, 1), :] = squares(qraw)
    k_in.wait()
    sum_out[pl.ds(1, 1), :] = squares(kraw)

    pl.semaphore_wait(barrier, 2 * (Z - 1) + 1)

    def sum_copy(d):
        return pltpu.make_async_remote_copy(
            src_ref=sum_out,
            dst_ref=sum_in.at[member],
            send_sem=sum_send.at[d - 1],
            recv_sem=sum_recv.at[member],
            device_id={"head": video + lax.rem(member + d, GROUP)},
            device_id_type=MESH,
        )

    def sum_arrival(d):
        slot = lax.rem(member + d, GROUP)
        return pltpu.make_async_remote_copy(
            src_ref=sum_out,
            dst_ref=sum_in.at[slot],
            send_sem=sum_send.at[d - 1],
            recv_sem=sum_recv.at[slot],
            device_id={"head": video + slot},
            device_id_type=MESH,
        )

    for d in range(1, GROUP):
        sum_copy(d).start()

    def piece(kind, d):
        to = column(d)
        stream, _ = owner_of(to, shift, core)
        src = (v_hbm, kn, qn)[kind].at[stream]
        dst = (vbuf.at[me], kbuf.at[me], qbuf.at[z])[kind]
        return pltpu.make_async_remote_copy(
            src_ref=src,
            dst_ref=dst,
            send_sem=kv_send.at[kind, d],
            recv_sem=kv_recv.at[kind, z],
            device_id={"seq": half * Z + to},
            device_id_type=MESH,
        )

    def own_piece(kind):
        src = (v_hbm, kn, qn)[kind].at[mine]
        dst = (vbuf.at[me], kbuf.at[me], qbuf.at[z])[kind]
        return pltpu.make_async_copy(src, dst, kv_recv.at[kind, z])

    def arrival(kind, d):
        slot = column(d)
        dst = (vbuf.at[half * Z + slot], kbuf.at[half * Z + slot], qbuf.at[slot])[kind]
        return pltpu.make_async_remote_copy(
            src_ref=dst,
            dst_ref=dst,
            send_sem=kv_send.at[kind, d],
            recv_sem=kv_recv.at[kind, slot],
            device_id={"seq": half * Z + slot},
            device_id_type=MESH,
        )

    def order_piece(d):
        to = column(d)
        stream, _ = owner_of(to, shift, core)
        return pltpu.make_async_remote_copy(
            src_ref=ord_out.at[stream],
            dst_ref=ord_in.at[half, z],
            send_sem=ord_send.at[d],
            recv_sem=ord_recv.at[z],
            device_id={"seq": half * Z + to},
            device_id_type=MESH,
        )

    def own_order():
        return pltpu.make_async_copy(ord_out.at[mine], ord_in.at[half, z], ord_recv.at[z])

    def order_arrival(d):
        slot = column(d)
        return pltpu.make_async_remote_copy(
            src_ref=ord_in.at[half, slot],
            dst_ref=ord_in.at[half, slot],
            send_sem=ord_send.at[d],
            recv_sem=ord_recv.at[slot],
            device_id={"seq": half * Z + slot},
            device_id_type=MESH,
        )

    def forward(kind, slot, side):
        buf = (vbuf, kbuf)[kind]
        return pltpu.make_async_remote_copy(
            src_ref=buf.at[side * Z + slot],
            dst_ref=buf.at[side * Z + slot],
            send_sem=fwd_send.at[kind, slot],
            recv_sem=fwd_recv.at[kind, slot],
            device_id=partner,
            device_id_type=MESH,
        )

    def order_forward(side):
        return pltpu.make_async_remote_copy(
            src_ref=ord_in.at[side],
            dst_ref=ord_in.at[side],
            send_sem=ofw_send.at[0],
            recv_sem=ofw_recv.at[0],
            device_id=partner,
            device_id_type=MESH,
        )

    def to_all(make):
        for d in FAR_FIRST[:-1]:
            _, there = owner_of(column(d), shift, core)

            @pl.when(there)
            def _(d=d):
                make(d)

    to_all(lambda d: order_piece(d).start())
    to_all(lambda d: piece(0, d).start())

    @pl.when(busy)
    def _():
        own_order().start()
        own_piece(0).start()

    total = sum_out[...]
    for d in range(1, GROUP):
        sum_arrival(d).wait_recv()
    for d in range(1, GROUP):
        total = total + sum_in[lax.rem(member + d, GROUP)]
    scale = lax.rsqrt(total * (1.0 / (HEADS * ROWS)) + EPS)

    def normalize(raw, gains, row, out):
        by_row = jnp.broadcast_to(scale[row : row + 1, :], (ROWS, ROWS)).T
        for j in range(STREAMS):
            gain = gains[pl.ds(member * STREAMS + j, 1), :]
            out[j] = (raw[j].astype(F32) * by_row * gain).astype(BF16)

    normalize(kraw, kg_ref, 1, kn)
    normalize(qraw, qg_ref, 0, qn)
    to_all(lambda d: piece(1, d).start())
    to_all(lambda d: piece(2, d).start())

    def result(slot):
        return pltpu.make_async_remote_copy(
            src_ref=obuf.at[slot],
            dst_ref=out_ref.at[mine],
            send_sem=out_send.at[slot],
            recv_sem=out_recv.at[mine],
            device_id={"seq": half * Z + slot},
            device_id_type=MESH,
        )

    def own_result():
        return pltpu.make_async_copy(obuf.at[z], out_ref.at[mine], out_recv.at[mine])

    def result_arrival(d):
        stream, _ = owner_of(column(d), shift, core)
        return pltpu.make_async_remote_copy(
            src_ref=obuf.at[0],
            dst_ref=out_ref.at[stream],
            send_sem=out_send.at[0],
            recv_sem=out_recv.at[stream],
            device_id={"seq": half * Z + column(d)},
            device_id_type=MESH,
        )

    @pl.when(busy)
    def _():
        own_piece(1).start()
        own_piece(2).start()
        own_order().wait()
        for d in NEAR_FIRST[1:]:
            order_arrival(d).wait_recv()
        order_forward(half).start()
        own_piece(0).wait()
        forward(0, z, half).start()
        for d in NEAR_FIRST[1:]:
            arrival(0, d).wait_recv()
            forward(0, column(d), half).start()
        own_piece(1).wait()
        forward(1, z, half).start()
        for d in NEAR_FIRST[1:]:
            arrival(1, d).wait_recv()
            forward(1, column(d), half).start()

        order_forward(1 - half).wait_recv()
        tokens = ord_in[:, :, 0, :].reshape(CLUSTERS, ROWS)
        place = lax.broadcasted_iota(jnp.int32, (CLUSTERS, ROWS), 0) * ROWS
        place = place + lax.broadcasted_iota(jnp.int32, (CLUSTERS, ROWS), 1)
        owner = jnp.full((CLUSTERS, ROWS), -1, jnp.int32)
        start = jnp.zeros((CLUSTERS, ROWS), jnp.int32)
        at = jnp.int32(0)
        for o in range(CLUSTERS):
            begun = place >= at
            owner = owner + begun.astype(jnp.int32)
            start = jnp.where(begun, at, start)
            at = at + rows_ref[mine, o]
        block = (owner * 2 + jnp.right_shift(place - start, 7)).astype(F32)
        high = jnp.right_shift(tokens, 7)
        low = jnp.bitwise_and(tokens, ROWS - 1)
        digit = lax.broadcasted_iota(jnp.int32, (ROWS, ROWS), 0)
        digit_high = lax.broadcasted_iota(jnp.int32, (CLUSTERS, ROWS), 0)
        for i in range(CLUSTERS):
            span = pl.ds(i * ROWS, ROWS)
            hit = digit == jnp.broadcast_to(low[i : i + 1], (ROWS, ROWS))
            bt_scr[:, span] = jnp.where(hit, 1.0, 0.0).astype(BF16)
            hit = digit_high == jnp.broadcast_to(high[i : i + 1], (CLUSTERS, ROWS))
            here = jnp.broadcast_to(block[i : i + 1], (CLUSTERS, ROWS))
            a_scr[:, span] = jnp.where(hit, here, 0.0).astype(BF16)
        by_low = lax.dot_general(
            bt_scr[...], a_scr[...], (((1,), (1,)), ((), ())), preferred_element_type=F32
        ).astype(BF16)
        lane = lax.broadcasted_iota(jnp.int32, (CLUSTERS, ROWS * CLUSTERS), 1)
        spread = jnp.right_shift(lane, 7) == lax.broadcasted_iota(
            jnp.int32, (CLUSTERS, ROWS * CLUSTERS), 0
        )
        wide = jnp.dot(
            by_low, jnp.where(spread, 1.0, 0.0).astype(BF16), preferred_element_type=F32
        )
        which = lax.broadcasted_iota(jnp.int32, (ROWS, ROWS), 1).astype(F32)
        for i in range(CLUSTERS):
            hit = wide[:, i * ROWS : (i + 1) * ROWS] == which
            oht[i] = jnp.where(hit, 1.0, 0.0).astype(BF16)
        mbuf[...] = jnp.zeros((ROWS, ROWS), BF16)
        same = lax.broadcasted_iota(jnp.int32, (BLOCKS, BLOCKS), 0) == (
            lax.broadcasted_iota(jnp.int32, (BLOCKS, BLOCKS), 1)
        )
        open_ = jnp.logical_or(map_ref[mine] == 1, same)
        mbuf[pl.ds(0, BLOCKS), pl.ds(0, BLOCKS)] = jnp.where(open_, 0.0, MASKED).astype(BF16)

        own_piece(2).wait()
        for d in NEAR_FIRST[1:]:
            arrival(2, d).wait_recv()
        for kind in range(2):
            for d in NEAR_FIRST:
                forward(kind, column(d), 1 - half).wait_recv()

        factor = math.log2(math.e) / math.sqrt(ROWS)
        chunks = CLUSTERS * ROWS // KEY_CHUNK
        per = KEY_CHUNK // ROWS

        def unit(t, carry):
            d = 4 + (1 - 2 * lax.rem(t, 2)) * ((t + 1) // 2)
            slot = column(d)
            bias = jnp.dot(oht[half * Z + slot], mbuf[...], preferred_element_type=F32)
            left = jnp.concatenate([qbuf[slot], bias.astype(BF16)], axis=1)
            peak = jnp.full((ROWS, 1), -jnp.inf, F32)
            for i in range(chunks):
                keys = kbuf[pl.ds(i * per, per)].reshape(KEY_CHUNK, ROWS)
                tags = oht[pl.ds(i * per, per)].reshape(KEY_CHUNK, ROWS)
                scores = lax.dot_general(
                    left,
                    jnp.concatenate([keys, tags], axis=1),
                    (((1,), (1,)), ((), ())),
                    preferred_element_type=F32,
                )
                s_scr[:, pl.ds(i * KEY_CHUNK, KEY_CHUNK)] = scores
                peak = jnp.maximum(peak, jnp.max(scores, axis=1, keepdims=True))
            denom = jnp.zeros((ROWS, 1), F32)
            mixed = jnp.zeros((ROWS, ROWS), F32)
            for i in range(chunks):
                p = jnp.exp2((s_scr[:, pl.ds(i * KEY_CHUNK, KEY_CHUNK)] - peak) * factor)
                denom = denom + jnp.sum(p, axis=1, keepdims=True)
                values = vbuf[pl.ds(i * per, per)].reshape(KEY_CHUNK, ROWS)
                mixed = mixed + jnp.dot(p.astype(BF16), values, preferred_element_type=F32)
            obuf[slot] = (mixed / denom).astype(BF16)

            @pl.when(t < Z - 1)
            def _():
                result(slot).start()

            return carry

        lax.fori_loop(0, Z, unit, 0)
        own_result().start()

    for d in range(1, GROUP):
        sum_copy(d).wait_send()
    to_all(lambda d: order_piece(d).wait_send())
    for kind in range(3):
        to_all(lambda d, kind=kind: piece(kind, d).wait_send())

    @pl.when(busy)
    def _():
        order_forward(half).wait_send()
        for kind in range(2):
            for d in NEAR_FIRST:
                forward(kind, column(d), half).wait_send()
        for d in FAR_FIRST[:-1]:
            result(column(d)).wait_send()
        own_result().wait()

    to_all(lambda d: result_arrival(d).wait_recv())


def local(query, key, value, q_gain, k_gain, order, cluster_rows, block_map):
    streams = query.shape[0]
    any_ = pl.BlockSpec(memory_space=pl.ANY)
    vmem = pl.BlockSpec(memory_space=pltpu.VMEM)
    smem = pl.BlockSpec(memory_space=pltpu.SMEM)
    sems = pltpu.SemaphoreType.DMA
    return pl.pallas_call(
        kernel,
        out_shape=jax.ShapeDtypeStruct((streams, ROWS, ROWS), BF16),
        in_specs=[any_, any_, any_, vmem, vmem, vmem, smem, vmem],
        out_specs=any_,
        scratch_shapes=[
            pltpu.VMEM((STREAMS, ROWS, ROWS), BF16),
            pltpu.VMEM((STREAMS, ROWS, ROWS), BF16),
            pltpu.VMEM((STREAMS, ROWS, ROWS), BF16),
            pltpu.VMEM((STREAMS, ROWS, ROWS), BF16),
            pltpu.VMEM((8, ROWS), F32),
            pltpu.VMEM((GROUP, 8, ROWS), F32),
            pltpu.VMEM((STREAMS, 8, ROWS), jnp.int32),
            pltpu.VMEM((2, Z, 8, ROWS), jnp.int32),
            pltpu.VMEM((2 * Z, ROWS, ROWS), BF16),
            pltpu.VMEM((2 * Z, ROWS, ROWS), BF16),
            pltpu.VMEM((Z, ROWS, ROWS), BF16),
            pltpu.VMEM((Z, ROWS, ROWS), BF16),
            pltpu.VMEM((2 * Z, ROWS, ROWS), BF16),
            pltpu.VMEM((ROWS, ROWS), BF16),
            pltpu.VMEM((ROWS, 2 * Z * ROWS), F32),
            pltpu.VMEM((ROWS, 2 * Z * ROWS), BF16),
            pltpu.VMEM((CLUSTERS, 2 * Z * ROWS), BF16),
            sems((2,)),
            sems((GROUP - 1,)),
            sems((GROUP,)),
            sems((Z,)),
            sems((Z,)),
            sems((3, Z)),
            sems((3, Z)),
            sems((2, Z)),
            sems((2, Z)),
            sems((1,)),
            sems((1,)),
            sems((Z,)),
            sems((STREAMS,)),
        ],
        compiler_params=pltpu.CompilerParams(collective_id=0, has_side_effects=True),
        name="attend",
    )(query, key, value, q_gain, k_gain, order, cluster_rows, block_map)


def solution(mesh):
    return jax.shard_map(
        local,
        mesh=mesh,
        in_specs=(
            P("head", "seq", None),
            P("head", "seq", None),
            P("head", "seq", None),
            P(),
            P(),
            P("head", "seq"),
            P("head", None),
            P("head", None, None),
        ),
        out_specs=P("head", "seq", None),
        check_vma=False,
    )
```

time: 184 us -> 45.1 us (0.25)
  the two profiles are of different devices: /device:TPU:1 before, /device:TPU:74 now
where the time goes in v1:
time: 45.1 us; the launch traced here: 44.9 us
  Pallas kernels  43.3 us (96%)
  local copies, waits for them, and re-layouts  1.59 us (4%)
    pallas_call x1, Pallas kernels, local(): pl.pallas_call(kernel, out_shape=jax.ShapeDtypeStruct((streams, ROWS, ROW...  43.3 us
    unnamed x1, local copies, waits for them, and re-layouts  1.59 us

profile of v1, /device:TPU:74, one launch (start us, length us, event | category | flops | bytes accessed | tf_op | source)
XLA Modules:
  0.0 44.9 jit_solution(8508629735840397586)
XLA Ops:
  0.0 43.3 %attend.1 = bf16[5,128,128]{2,1,0:T(8,128)(2,1)} custom-call(bf16[5,128,128]{2,1,0:T(8,128)(2,1)} %q_hbm.1, bf16[5,128,128]{2,1,0:T(8,128)(2,1)} %k_hbm.1, bf16[5,128,128]{2,1,0:T(8,128)(2,1)} %v_hbm.1, f32[40,128]{1,0:T(8,128)} %qg_ref.1, f32[40,128]{1,0:T(8,128)} %kg_ref.1, s32[5,128]{1,0:T(8,128)} %order_ref.1, s32[5,16]{1,0:T(8,128)} %rows_ref.1, ...), custom_call_target="tpu_custom_call" | custom-call | tf_op jit(solution)/shard_map/attend/pallas_call | solution.py:385
  43.3 1.6 %copy.10 = bf16[5,128,128]{2,1,0:T(8,128)(2,1)} copy(bf16[5,128,128]{2,1,0:T(8,128)(2,1)} %attend.1) | data formatting | bytes 327680

commit v2 on v1

v2 whole, which is shorter than its diff:
```python
import math

import jax
import jax.numpy as jnp
from jax import lax
from jax.experimental import pallas as pl
from jax.experimental.pallas import tpu as pltpu
from jax.sharding import PartitionSpec as P

MESH = pl.DeviceIdType.MESH
F32 = jnp.float32
BF16 = jnp.bfloat16

EPS = 1e-06
ROWS = 128
Z = 8
STREAMS = 5
HEADS = 40
GROUP = 8
CLUSTERS = 16
BLOCKS = 32
MASKED = -(2.0**30)
FAR_FIRST = (4, 3, 5, 2, 6, 1, 7, 0)
KEY_CHUNK = 512
PER = KEY_CHUNK // ROWS
PARTS = Z // PER


def owner_of(z, shift, core):
    v = lax.rem(z - shift + 3 * core + 16, Z)
    stream = jnp.minimum(v - 3 * core * (v // 7), STREAMS - 1)
    busy = jnp.logical_or(v < STREAMS - core, core * v == 7)
    return stream, busy


def kernel(
    q_hbm, k_hbm, v_hbm, qg_hbm, kg_hbm, order_hbm, rows_hbm, map_hbm, out_ref,
    qg_ref, kg_ref, order_ref, rows_ref, map_ref, qraw, kraw, qn, kn, sum_out, sum_in, ord_out, ord_in, kbuf, vbuf, qbuf, obuf,
    oht, mbuf, lbuf, peaks, denoms, mixes, s_scr, bt_scr, a_scr,
    raw_sem, sum_send, sum_recv, ord_send, ord_recv, kv_send, kv_recv, fwd_send, fwd_recv,
    ofw_send, ofw_recv, out_send, out_recv,
):
    me = lax.axis_index("seq")
    head = lax.axis_index("head")
    half, z = me // Z, lax.rem(me, Z)
    shift = 2 * lax.rem(head // 2, 2)
    core = lax.rem(head, 2)
    member = lax.rem(head, GROUP)
    video = head - member
    mine, busy = owner_of(z, shift, core)
    partner = {"seq": (1 - half) * Z + z}

    def column(d):
        return lax.rem(z + d, Z)

    barrier = pltpu.get_barrier_semaphore()
    for d in range(1, Z):
        pl.semaphore_signal(
            barrier, inc=1, device_id={"seq": half * Z + column(d)}, device_id_type=MESH
        )
        pl.semaphore_signal(
            barrier,
            inc=1,
            device_id={"head": video + lax.rem(member + d, GROUP)},
            device_id_type=MESH,
        )
    pl.semaphore_signal(barrier, inc=1, device_id=partner, device_id_type=MESH)

    q_in = pltpu.make_async_copy(q_hbm, qraw, raw_sem.at[0])
    k_in = pltpu.make_async_copy(k_hbm, kraw, raw_sem.at[1])
    small = [
        pltpu.make_async_copy(src, dst, raw_sem.at[2 + i])
        for i, (src, dst) in enumerate(
            (
                (order_hbm, order_ref),
                (kg_hbm, kg_ref),
                (qg_hbm, qg_ref),
                (rows_hbm, rows_ref),
                (map_hbm, map_ref),
            )
        )
    ]
    small[0].start()
    q_in.start()
    k_in.start()
    for copy in small[1:]:
        copy.start()
    pl.semaphore_wait(barrier, 2 * (Z - 1) + 1)

    def sum_copy(d):
        return pltpu.make_async_remote_copy(
            src_ref=sum_out,
            dst_ref=sum_in.at[member],
            send_sem=sum_send.at[d - 1],
            recv_sem=sum_recv.at[member],
            device_id={"head": video + lax.rem(member + d, GROUP)},
            device_id_type=MESH,
        )

    def sum_arrival(d):
        slot = lax.rem(member + d, GROUP)
        return pltpu.make_async_remote_copy(
            src_ref=sum_out,
            dst_ref=sum_in.at[slot],
            send_sem=sum_send.at[d - 1],
            recv_sem=sum_recv.at[slot],
            device_id={"head": video + slot},
            device_id_type=MESH,
        )

    def piece(kind, d):
        to = column(d)
        stream, _ = owner_of(to, shift, core)
        src = (v_hbm, kn, qn)[kind].at[stream]
        dst = (vbuf.at[me], kbuf.at[me], qbuf.at[z])[kind]
        return pltpu.make_async_remote_copy(
            src_ref=src,
            dst_ref=dst,
            send_sem=kv_send.at[kind, d],
            recv_sem=kv_recv.at[kind, z],
            device_id={"seq": half * Z + to},
            device_id_type=MESH,
        )

    def own_piece(kind):
        src = (v_hbm, kn, qn)[kind].at[mine]
        dst = (vbuf.at[me], kbuf.at[me], qbuf.at[z])[kind]
        return pltpu.make_async_copy(src, dst, kv_recv.at[kind, z])

    def arrival(kind, d):
        slot = column(d)
        dst = (vbuf.at[half * Z + slot], kbuf.at[half * Z + slot], qbuf.at[slot])[kind]
        return pltpu.make_async_remote_copy(
            src_ref=dst,
            dst_ref=dst,
            send_sem=kv_send.at[kind, d],
            recv_sem=kv_recv.at[kind, slot],
            device_id={"seq": half * Z + slot},
            device_id_type=MESH,
        )

    def order_piece(d):
        to = column(d)
        stream, _ = owner_of(to, shift, core)
        return pltpu.make_async_remote_copy(
            src_ref=ord_out.at[stream],
            dst_ref=ord_in.at[half, z],
            send_sem=ord_send.at[d],
            recv_sem=ord_recv.at[z],
            device_id={"seq": half * Z + to},
            device_id_type=MESH,
        )

    def own_order():
        return pltpu.make_async_copy(ord_out.at[mine], ord_in.at[half, z], ord_recv.at[z])

    def order_arrival(d):
        slot = column(d)
        return pltpu.make_async_remote_copy(
            src_ref=ord_in.at[half, slot],
            dst_ref=ord_in.at[half, slot],
            send_sem=ord_send.at[d],
            recv_sem=ord_recv.at[slot],
            device_id={"seq": half * Z + slot},
            device_id_type=MESH,
        )

    def forward(kind, slot, side):
        buf = (vbuf, kbuf)[kind]
        return pltpu.make_async_remote_copy(
            src_ref=buf.at[side * Z + slot],
            dst_ref=buf.at[side * Z + slot],
            send_sem=fwd_send.at[kind, slot],
            recv_sem=fwd_recv.at[kind, slot],
            device_id=partner,
            device_id_type=MESH,
        )

    def order_forward(side):
        return pltpu.make_async_remote_copy(
            src_ref=ord_in.at[side],
            dst_ref=ord_in.at[side],
            send_sem=ofw_send.at[0],
            recv_sem=ofw_recv.at[0],
            device_id=partner,
            device_id_type=MESH,
        )

    def to_all(make):
        for d in FAR_FIRST[:-1]:
            _, there = owner_of(column(d), shift, core)

            @pl.when(there)
            def _(d=d):
                make(d)

    to_all(lambda d: piece(0, d).start())
    small[0].wait()
    sum_out[...] = jnp.zeros((8, ROWS), F32)
    for j in range(STREAMS):
        ord_out[j] = jnp.broadcast_to(order_ref[pl.ds(j, 1), :], (8, ROWS))

    def squares(raw):
        total = jnp.zeros((ROWS, ROWS), F32)
        for j in range(STREAMS):
            x = raw[j].astype(F32)
            total = total + x * x
        return jnp.sum(total.T, axis=0, keepdims=True)
    to_all(lambda d: order_piece(d).start())

    @pl.when(busy)
    def _():
        own_order().start()
        own_piece(0).start()

    q_in.wait()
    sum_out[pl.ds(0, 1), :] = squares(qraw)
    k_in.wait()
    sum_out[pl.ds(1, 1), :] = squares(kraw)
    for d in range(1, GROUP):
        sum_copy(d).start()
    for copy in small[1:]:
        copy.wait()
    total = sum_out[...]
    for d in range(1, GROUP):
        sum_arrival(d).wait_recv()
    for d in range(1, GROUP):
        total = total + sum_in[lax.rem(member + d, GROUP)]
    scale = lax.rsqrt(total * (1.0 / (HEADS * ROWS)) + EPS)

    def by_row(row):
        return jnp.broadcast_to(scale[row : row + 1, :], (ROWS, ROWS)).T

    def normalize(kind, d, rows):
        stream, _ = owner_of(column(d), shift, core)
        raw, gains, out = ((kraw, kg_ref, kn), (qraw, qg_ref, qn))[kind - 1]
        gain = gains[pl.ds(member * STREAMS + stream, 1), :]
        out[stream] = (raw[stream].astype(F32) * rows * gain).astype(BF16)

    for kind in (1, 2):
        rows = by_row(2 - kind)

        def ready(d, kind=kind, rows=rows):
            normalize(kind, d, rows)
            piece(kind, d).start()

        to_all(ready)

        @pl.when(busy)
        def _(kind=kind, rows=rows):
            normalize(kind, 0, rows)
            own_piece(kind).start()

    def result(slot):
        return pltpu.make_async_remote_copy(
            src_ref=obuf.at[slot],
            dst_ref=out_ref.at[mine],
            send_sem=out_send.at[slot],
            recv_sem=out_recv.at[mine],
            device_id={"seq": half * Z + slot},
            device_id_type=MESH,
        )

    def own_result():
        return pltpu.make_async_copy(obuf.at[z], out_ref.at[mine], out_recv.at[mine])

    def result_arrival(d):
        stream, _ = owner_of(column(d), shift, core)
        return pltpu.make_async_remote_copy(
            src_ref=obuf.at[0],
            dst_ref=out_ref.at[stream],
            send_sem=out_send.at[0],
            recv_sem=out_recv.at[stream],
            device_id={"seq": half * Z + column(d)},
            device_id_type=MESH,
        )

    @pl.when(busy)
    def _():
        own_piece(0).wait()
        forward(0, z, half).start()
        for d in FAR_FIRST[:-1]:
            arrival(0, d).wait_recv()
            forward(0, column(d), half).start()
        own_order().wait()
        for d in FAR_FIRST[:-1]:
            order_arrival(d).wait_recv()
        order_forward(half).start()
        own_piece(1).wait()
        forward(1, z, half).start()
        for d in FAR_FIRST[:-1]:
            arrival(1, d).wait_recv()
            forward(1, column(d), half).start()

        order_forward(1 - half).wait_recv()
        tokens = ord_in[:, :, 0, :].reshape(CLUSTERS, ROWS)
        place = lax.broadcasted_iota(jnp.int32, (CLUSTERS, ROWS), 0) * ROWS
        place = place + lax.broadcasted_iota(jnp.int32, (CLUSTERS, ROWS), 1)
        owner = jnp.full((CLUSTERS, ROWS), -1, jnp.int32)
        start = jnp.zeros((CLUSTERS, ROWS), jnp.int32)
        at = jnp.int32(0)
        for o in range(CLUSTERS):
            begun = place >= at
            owner = owner + begun.astype(jnp.int32)
            start = jnp.where(begun, at, start)
            at = at + rows_ref[mine, o]
        block = (owner * 2 + jnp.right_shift(place - start, 7)).astype(F32)
        high = jnp.right_shift(tokens, 7)
        low = jnp.bitwise_and(tokens, ROWS - 1)
        digit = lax.broadcasted_iota(jnp.int32, (ROWS, ROWS), 0)
        digit_high = lax.broadcasted_iota(jnp.int32, (CLUSTERS, ROWS), 0)
        for i in range(CLUSTERS):
            span = pl.ds(i * ROWS, ROWS)
            hit = digit == jnp.broadcast_to(low[i : i + 1], (ROWS, ROWS))
            bt_scr[:, span] = jnp.where(hit, 1.0, 0.0).astype(BF16)
            hit = digit_high == jnp.broadcast_to(high[i : i + 1], (CLUSTERS, ROWS))
            here = jnp.broadcast_to(block[i : i + 1], (CLUSTERS, ROWS))
            a_scr[:, span] = jnp.where(hit, here, 0.0).astype(BF16)
        by_low = lax.dot_general(
            bt_scr[...], a_scr[...], (((1,), (1,)), ((), ())), preferred_element_type=F32
        ).astype(BF16)
        lane = lax.broadcasted_iota(jnp.int32, (CLUSTERS, ROWS * CLUSTERS), 1)
        spread = jnp.right_shift(lane, 7) == lax.broadcasted_iota(
            jnp.int32, (CLUSTERS, ROWS * CLUSTERS), 0
        )
        wide = jnp.dot(
            by_low, jnp.where(spread, 1.0, 0.0).astype(BF16), preferred_element_type=F32
        )
        which = lax.broadcasted_iota(jnp.int32, (ROWS, ROWS), 1).astype(F32)
        for i in range(CLUSTERS):
            hit = wide[:, i * ROWS : (i + 1) * ROWS] == which
            oht[i] = jnp.where(hit, 1.0, 0.0).astype(BF16)
        mbuf[...] = jnp.zeros((ROWS, ROWS), BF16)
        same = lax.broadcasted_iota(jnp.int32, (BLOCKS, BLOCKS), 0) == (
            lax.broadcasted_iota(jnp.int32, (BLOCKS, BLOCKS), 1)
        )
        open_ = jnp.logical_or(map_ref[mine] == 1, same)
        mbuf[pl.ds(0, BLOCKS), pl.ds(0, BLOCKS)] = jnp.where(open_, 0.0, MASKED).astype(BF16)

        factor = math.log2(math.e) / math.sqrt(ROWS)

        def weigh(left, side, start):
            peak = start
            for i in range(PARTS):
                span = pl.ds(side * Z + i * PER, PER)
                scores = lax.dot_general(
                    left,
                    jnp.concatenate(
                        [
                            kbuf[span].reshape(KEY_CHUNK, ROWS),
                            oht[span].reshape(KEY_CHUNK, ROWS),
                        ],
                        axis=1,
                    ),
                    (((1,), (1,)), ((), ())),
                    preferred_element_type=F32,
                )
                s_scr[:, pl.ds(i * KEY_CHUNK, KEY_CHUNK)] = scores
                peak = jnp.maximum(peak, jnp.max(scores, axis=1, keepdims=True))
            denom = jnp.zeros((2 * ROWS, 1), F32)
            mixed = jnp.zeros((2 * ROWS, ROWS), F32)
            for i in range(PARTS):
                span = pl.ds(side * Z + i * PER, PER)
                p = jnp.exp2((s_scr[:, pl.ds(i * KEY_CHUNK, KEY_CHUNK)] - peak) * factor)
                denom = denom + jnp.sum(p, axis=1, keepdims=True)
                values = vbuf[span].reshape(KEY_CHUNK, ROWS)
                mixed = mixed + jnp.dot(p.astype(BF16), values, preferred_element_type=F32)
            return peak, denom, mixed

        def near_half(t, carry):
            first, second = lax.rem(4 - t, 4), 4 + t

            @pl.when(t == 0)
            def _():
                own_piece(2).wait()

            @pl.when(t > 0)
            def _():
                arrival(2, first).wait_recv()

            arrival(2, second).wait_recv()
            lefts = []
            for d in (first, second):
                slot = column(d)
                bias = jnp.dot(oht[half * Z + slot], mbuf[...], preferred_element_type=F32)
                left = jnp.concatenate([qbuf[slot], bias.astype(BF16)], axis=1)
                lbuf[slot] = left
                lefts.append(left)
            peak, denom, mixed = weigh(
                jnp.concatenate(lefts, axis=0), half, jnp.full((2 * ROWS, 1), -jnp.inf, F32)
            )
            for i, d in enumerate((first, second)):
                slot = column(d)
                rows = slice(i * ROWS, (i + 1) * ROWS)
                peaks[slot] = peak[rows]
                denoms[slot] = denom[rows]
                mixes[slot] = mixed[rows]
            return carry

        def far_half(t, carry):
            slots = (column(4 + t), column(3 - t))
            left = jnp.concatenate([lbuf[slot] for slot in slots], axis=0)
            before = jnp.concatenate([peaks[slot] for slot in slots], axis=0)
            peak, denom, mixed = weigh(left, 1 - half, before)
            fade = jnp.exp2((before - peak) * factor)
            denom = denom + fade * jnp.concatenate([denoms[slot] for slot in slots], axis=0)
            mixed = mixed + fade * jnp.concatenate([mixes[slot] for slot in slots], axis=0)
            out = (mixed / denom).astype(BF16)
            for i, slot in enumerate(slots):
                obuf[slot] = out[i * ROWS : (i + 1) * ROWS]
            result(slots[0]).start()

            @pl.when(t < 3)
            def _():
                result(slots[1]).start()

            return carry

        lax.fori_loop(0, Z // 2, near_half, 0)
        for kind in range(2):
            for d in FAR_FIRST:
                forward(kind, column(d), 1 - half).wait_recv()
        lax.fori_loop(0, Z // 2, far_half, 0)
        own_result().start()

    for d in range(1, GROUP):
        sum_copy(d).wait_send()
    to_all(lambda d: order_piece(d).wait_send())
    for kind in range(3):
        to_all(lambda d, kind=kind: piece(kind, d).wait_send())

    @pl.when(busy)
    def _():
        order_forward(half).wait_send()
        for kind in range(2):
            for d in FAR_FIRST:
                forward(kind, column(d), half).wait_send()
        for d in FAR_FIRST[:-1]:
            result(column(d)).wait_send()
        own_result().wait()

    to_all(lambda d: result_arrival(d).wait_recv())


def local(query, key, value, q_gain, k_gain, order, cluster_rows, block_map):
    streams = query.shape[0]
    any_ = pl.BlockSpec(memory_space=pl.ANY)
    sems = pltpu.SemaphoreType.DMA
    return pl.pallas_call(
        kernel,
        out_shape=pltpu.VMEM((streams, ROWS, ROWS), BF16),
        in_specs=[any_] * 8,
        out_specs=pl.BlockSpec(memory_space=pltpu.VMEM),
        scratch_shapes=[
            pltpu.VMEM((HEADS, ROWS), F32),
            pltpu.VMEM((HEADS, ROWS), F32),
            pltpu.VMEM((STREAMS, ROWS), jnp.int32),
            pltpu.SMEM((STREAMS, CLUSTERS), jnp.int32),
            pltpu.VMEM((STREAMS, BLOCKS, BLOCKS), jnp.int32),
            pltpu.VMEM((STREAMS, ROWS, ROWS), BF16),
            pltpu.VMEM((STREAMS, ROWS, ROWS), BF16),
            pltpu.VMEM((STREAMS, ROWS, ROWS), BF16),
            pltpu.VMEM((STREAMS, ROWS, ROWS), BF16),
            pltpu.VMEM((8, ROWS), F32),
            pltpu.VMEM((GROUP, 8, ROWS), F32),
            pltpu.VMEM((STREAMS, 8, ROWS), jnp.int32),
            pltpu.VMEM((2, Z, 8, ROWS), jnp.int32),
            pltpu.VMEM((2 * Z, ROWS, ROWS), BF16),
            pltpu.VMEM((2 * Z, ROWS, ROWS), BF16),
            pltpu.VMEM((Z, ROWS, ROWS), BF16),
            pltpu.VMEM((Z, ROWS, ROWS), BF16),
            pltpu.VMEM((2 * Z, ROWS, ROWS), BF16),
            pltpu.VMEM((ROWS, ROWS), BF16),
            pltpu.VMEM((Z, ROWS, 2 * ROWS), BF16),
            pltpu.VMEM((Z, ROWS, 1), F32),
            pltpu.VMEM((Z, ROWS, 1), F32),
            pltpu.VMEM((Z, ROWS, ROWS), F32),
            pltpu.VMEM((2 * ROWS, Z * ROWS), F32),
            pltpu.VMEM((ROWS, 2 * Z * ROWS), BF16),
            pltpu.VMEM((CLUSTERS, 2 * Z * ROWS), BF16),
            sems((7,)),
            sems((GROUP - 1,)),
            sems((GROUP,)),
            sems((Z,)),
            sems((Z,)),
            sems((3, Z)),
            sems((3, Z)),
            sems((2, Z)),
            sems((2, Z)),
            sems((1,)),
            sems((1,)),
            sems((Z,)),
            sems((STREAMS,)),
        ],
        compiler_params=pltpu.CompilerParams(collective_id=0, has_side_effects=True),
        name="attend",
    )(query, key, value, q_gain, k_gain, order, cluster_rows, block_map)


def solution(mesh):
    return jax.shard_map(
        local,
        mesh=mesh,
        in_specs=(
            P("head", "seq", None),
            P("head", "seq", None),
            P("head", "seq", None),
            P(),
            P(),
            P("head", "seq"),
            P("head", None),
            P("head", None, None),
        ),
        out_specs=P("head", "seq", None),
        check_vma=False,
    )
```

time: 45.1 us -> 39.2 us (0.87)
  the two profiles are of different devices: /device:TPU:74 before, /device:TPU:1 now
where the time goes in v2:
time: 39.2 us; the launch traced here: 39 us
  Pallas kernels  38.3 us (98%)
  local copies, waits for them, and re-layouts  0.67 us (2%)
    pallas_call x1, Pallas kernels, local(): pl.pallas_call(kernel, out_shape=pltpu.VMEM((streams, ROWS, ROWS), BF16),...  38.3 us

profile of v2, /device:TPU:1, one launch (start us, length us, event | category | flops | bytes accessed | tf_op | source)
XLA Modules:
  0.0 39.0 jit_solution(4019766783634050003)
XLA Ops:
  0.0 38.3 %attend.1 = bf16[5,128,128]{2,1,0:T(8,128)(2,1)S(1)} custom-call(bf16[5,128,128]{2,1,0:T(8,128)(2,1)} %q_hbm.1, bf16[5,128,128]{2,1,0:T(8,128)(2,1)} %k_hbm.1, bf16[5,128,128]{2,1,0:T(8,128)(2,1)} %v_hbm.1, f32[40,128]{1,0:T(8,128)} %qg_hbm.1, f32[40,128]{1,0:T(8,128)} %kg_hbm.1, s32[5,128]{1,0:T(8,128)} %order_hbm.1, s32[5,16]{1,0:T(8,128)} %rows_hbm.1, ...), custom_call_target="tpu_custom_call" | custom-call | tf_op jit(solution)/shard_map/attend/pallas_call | solution.py:449
  38.3 0.7 %copy.10 = bf16[5,128,128]{2,1,0:T(8,128)(2,1)} copy(bf16[5,128,128]{2,1,0:T(8,128)(2,1)S(1)} %attend.1) | data formatting | bytes 327680

commit v3 on v2

--- a/solution.py
+++ b/solution.py
@@ -85,140 +85,141 @@
     k_in.start()
     for copy in small[1:]:
         copy.start()
-    pl.semaphore_wait(barrier, 2 * (Z - 1) + 1)
-
-    def sum_copy(d):
-        return pltpu.make_async_remote_copy(
-            src_ref=sum_out,
-            dst_ref=sum_in.at[member],
-            send_sem=sum_send.at[d - 1],
-            recv_sem=sum_recv.at[member],
-            device_id={"head": video + lax.rem(member + d, GROUP)},
-            device_id_type=MESH,
-        )
-
-    def sum_arrival(d):
-        slot = lax.rem(member + d, GROUP)
-        return pltpu.make_async_remote_copy(
-            src_ref=sum_out,
-            dst_ref=sum_in.at[slot],
-            send_sem=sum_send.at[d - 1],
-            recv_sem=sum_recv.at[slot],
-            device_id={"head": video + slot},
-            device_id_type=MESH,
-        )
-
-    def piece(kind, d):
-        to = column(d)
-        stream, _ = owner_of(to, shift, core)
-        src = (v_hbm, kn, qn)[kind].at[stream]
-        dst = (vbuf.at[me], kbuf.at[me], qbuf.at[z])[kind]
-        return pltpu.make_async_remote_copy(
-            src_ref=src,
-            dst_ref=dst,
-            send_sem=kv_send.at[kind, d],
-            recv_sem=kv_recv.at[kind, z],
-            device_id={"seq": half * Z + to},
-            device_id_type=MESH,
-        )
-
-    def own_piece(kind):
-        src = (v_hbm, kn, qn)[kind].at[mine]
-        dst = (vbuf.at[me], kbuf.at[me], qbuf.at[z])[kind]
-        return pltpu.make_async_copy(src, dst, kv_recv.at[kind, z])
-
-    def arrival(kind, d):
-        slot = column(d)
-        dst = (vbuf.at[half * Z + slot], kbuf.at[half * Z + slot], qbuf.at[slot])[kind]
-        return pltpu.make_async_remote_copy(
-            src_ref=dst,
-            dst_ref=dst,
-            send_sem=kv_send.at[kind, d],
-            recv_sem=kv_recv.at[kind, slot],
-            device_id={"seq": half * Z + slot},
-            device_id_type=MESH,
-        )
-
-    def order_piece(d):
-        to = column(d)
-        stream, _ = owner_of(to, shift, core)
-        return pltpu.make_async_remote_copy(
-            src_ref=ord_out.at[stream],
-            dst_ref=ord_in.at[half, z],
-            send_sem=ord_send.at[d],
-            recv_sem=ord_recv.at[z],
-            device_id={"seq": half * Z + to},
-            device_id_type=MESH,
-        )
-
-    def own_order():
-        return pltpu.make_async_copy(ord_out.at[mine], ord_in.at[half, z], ord_recv.at[z])
-
-    def order_arrival(d):
-        slot = column(d)
-        return pltpu.make_async_remote_copy(
-            src_ref=ord_in.at[half, slot],
-            dst_ref=ord_in.at[half, slot],
-            send_sem=ord_send.at[d],
-            recv_sem=ord_recv.at[slot],
-            device_id={"seq": half * Z + slot},
-            device_id_type=MESH,
-        )
-
-    def forward(kind, slot, side):
-        buf = (vbuf, kbuf)[kind]
-        return pltpu.make_async_remote_copy(
-            src_ref=buf.at[side * Z + slot],
-            dst_ref=buf.at[side * Z + slot],
-            send_sem=fwd_send.at[kind, slot],
-            recv_sem=fwd_recv.at[kind, slot],
-            device_id=partner,
-            device_id_type=MESH,
-        )
-
-    def order_forward(side):
-        return pltpu.make_async_remote_copy(
-            src_ref=ord_in.at[side],
-            dst_ref=ord_in.at[side],
-            send_sem=ofw_send.at[0],
-            recv_sem=ofw_recv.at[0],
-            device_id=partner,
-            device_id_type=MESH,
-        )
-
-    def to_all(make):
-        for d in FAR_FIRST[:-1]:
-            _, there = owner_of(column(d), shift, core)
-
-            @pl.when(there)
-            def _(d=d):
-                make(d)
-
-    to_all(lambda d: piece(0, d).start())
-    small[0].wait()
-    sum_out[...] = jnp.zeros((8, ROWS), F32)
-    for j in range(STREAMS):
-        ord_out[j] = jnp.broadcast_to(order_ref[pl.ds(j, 1), :], (8, ROWS))
-
     def squares(raw):
         total = jnp.zeros((ROWS, ROWS), F32)
         for j in range(STREAMS):
             x = raw[j].astype(F32)
             total = total + x * x
         return jnp.sum(total.T, axis=0, keepdims=True)
+
+    sum_out[...] = jnp.zeros((8, ROWS), F32)
+    q_in.wait()
+    sum_out[pl.ds(0, 1), :] = squares(qraw)
+    k_in.wait()
+    sum_out[pl.ds(1, 1), :] = squares(kraw)
+    small[0].wait()
+    for j in range(STREAMS):
+        ord_out[j] = jnp.broadcast_to(order_ref[pl.ds(j, 1), :], (8, ROWS))
+
+    pl.semaphore_wait(barrier, 2 * (Z - 1) + 1)
+
+    def sum_copy(d):
+        return pltpu.make_async_remote_copy(
+            src_ref=sum_out,
+            dst_ref=sum_in.at[member],
+            send_sem=sum_send.at[d - 1],
+            recv_sem=sum_recv.at[member],
+            device_id={"head": video + lax.rem(member + d, GROUP)},
+            device_id_type=MESH,
+        )
+
+    def sum_arrival(d):
+        slot = lax.rem(member + d, GROUP)
+        return pltpu.make_async_remote_copy(
+            src_ref=sum_out,
+            dst_ref=sum_in.at[slot],
+            send_sem=sum_send.at[d - 1],
+            recv_sem=sum_recv.at[slot],
+            device_id={"head": video + slot},
+            device_id_type=MESH,
+        )
+
+    def piece(kind, d):
+        to = column(d)
+        stream, _ = owner_of(to, shift, core)
+        src = (v_hbm, kn, qn)[kind].at[stream]
+        dst = (vbuf.at[me], kbuf.at[me], qbuf.at[z])[kind]
+        return pltpu.make_async_remote_copy(
+            src_ref=src,
+            dst_ref=dst,
+            send_sem=kv_send.at[kind, d],
+            recv_sem=kv_recv.at[kind, z],
+            device_id={"seq": half * Z + to},
+            device_id_type=MESH,
+        )
+
+    def own_piece(kind):
+        src = (v_hbm, kn, qn)[kind].at[mine]
+        dst = (vbuf.at[me], kbuf.at[me], qbuf.at[z])[kind]
+        return pltpu.make_async_copy(src, dst, kv_recv.at[kind, z])
+
+    def arrival(kind, d):
+        slot = column(d)
+        dst = (vbuf.at[half * Z + slot], kbuf.at[half * Z + slot], qbuf.at[slot])[kind]
+        return pltpu.make_async_remote_copy(
+            src_ref=dst,
+            dst_ref=dst,
+            send_sem=kv_send.at[kind, d],
+            recv_sem=kv_recv.at[kind, slot],
+            device_id={"seq": half * Z + slot},
+            device_id_type=MESH,
+        )
+
+    def order_piece(d):
+        to = column(d)
+        stream, _ = owner_of(to, shift, core)
+        return pltpu.make_async_remote_copy(
+            src_ref=ord_out.at[stream],
+            dst_ref=ord_in.at[half, z],
+            send_sem=ord_send.at[d],
+            recv_sem=ord_recv.at[z],
+            device_id={"seq": half * Z + to},
+            device_id_type=MESH,
+        )
+
+    def own_order():
+        return pltpu.make_async_copy(ord_out.at[mine], ord_in.at[half, z], ord_recv.at[z])
+
+    def order_arrival(d):
+        slot = column(d)
+        return pltpu.make_async_remote_copy(
+            src_ref=ord_in.at[half, slot],
+            dst_ref=ord_in.at[half, slot],
+            send_sem=ord_send.at[d],
+            recv_sem=ord_recv.at[slot],
+            device_id={"seq": half * Z + slot},
+            device_id_type=MESH,
+        )
+
+    def forward(kind, slot, side):
+        buf = (vbuf, kbuf)[kind]
+        return pltpu.make_async_remote_copy(
+            src_ref=buf.at[side * Z + slot],
+            dst_ref=buf.at[side * Z + slot],
+            send_sem=fwd_send.at[kind, slot],
+            recv_sem=fwd_recv.at[kind, slot],
+            device_id=partner,
+            device_id_type=MESH,
+        )
+
+    def order_forward(side):
+        return pltpu.make_async_remote_copy(
+            src_ref=ord_in.at[side],
+            dst_ref=ord_in.at[side],
+            send_sem=ofw_send.at[0],
+            recv_sem=ofw_recv.at[0],
+            device_id=partner,
+            device_id_type=MESH,
+        )
+
+    def to_all(make):
+        for d in FAR_FIRST[:-1]:
+            _, there = owner_of(column(d), shift, core)
+
+            @pl.when(there)
+            def _(d=d):
+                make(d)
+
+    for d in range(1, GROUP):
+        sum_copy(d).start()
     to_all(lambda d: order_piece(d).start())
+    to_all(lambda d: piece(0, d).start())
 
     @pl.when(busy)
     def _():
         own_order().start()
         own_piece(0).start()
 
-    q_in.wait()
-    sum_out[pl.ds(0, 1), :] = squares(qraw)
-    k_in.wait()
-    sum_out[pl.ds(1, 1), :] = squares(kraw)
-    for d in range(1, GROUP):
-        sum_copy(d).start()
     for copy in small[1:]:
         copy.wait()
     total = sum_out[...]
@@ -277,18 +278,18 @@
 
     @pl.when(busy)
     def _():
+        own_order().wait()
+        for d in FAR_FIRST[:-1]:
+            order_arrival(d).wait_recv()
+        order_forward(half).start()
         own_piece(0).wait()
         forward(0, z, half).start()
         for d in FAR_FIRST[:-1]:
             arrival(0, d).wait_recv()
             forward(0, column(d), half).start()
-        own_order().wait()
-        for d in FAR_FIRST[:-1]:
-            order_arrival(d).wait_recv()
-        order_forward(half).start()
         own_piece(1).wait()
         forward(1, z, half).start()
-        for d in FAR_FIRST[:-1]:
+        for d in FAR_FIRST[:4]:
             arrival(1, d).wait_recv()
             forward(1, column(d), half).start()
 
@@ -337,6 +338,10 @@
         open_ = jnp.logical_or(map_ref[mine] == 1, same)
         mbuf[pl.ds(0, BLOCKS), pl.ds(0, BLOCKS)] = jnp.where(open_, 0.0, MASKED).astype(BF16)
 
+        for d in FAR_FIRST[4:-1]:
+            arrival(1, d).wait_recv()
+            forward(1, column(d), half).start()
+
         factor = math.log2(math.e) / math.sqrt(ROWS)
 
         def weigh(left, side, start):
@@ -367,18 +372,18 @@
                 mixed = mixed + jnp.dot(p.astype(BF16), values, preferred_element_type=F32)
             return peak, denom, mixed
 
-        def near_half(t, carry):
-            first, second = lax.rem(4 - t, 4), 4 + t
-
-            @pl.when(t == 0)
+        def near_half(t):
+            first, second = 4 + t, 3 - t
+            arrival(2, first).wait_recv()
+
+            @pl.when(t < 3)
+            def _():
+                arrival(2, second).wait_recv()
+
+            @pl.when(t == 3)
             def _():
                 own_piece(2).wait()
 
-            @pl.when(t > 0)
-            def _():
-                arrival(2, first).wait_recv()
-
-            arrival(2, second).wait_recv()
             lefts = []
             for d in (first, second):
                 slot = column(d)
@@ -395,9 +400,8 @@
                 peaks[slot] = peak[rows]
                 denoms[slot] = denom[rows]
                 mixes[slot] = mixed[rows]
-            return carry
-
-        def far_half(t, carry):
+
+        def far_half(t):
             slots = (column(4 + t), column(3 - t))
             left = jnp.concatenate([lbuf[slot] for slot in slots], axis=0)
             before = jnp.concatenate([peaks[slot] for slot in slots], axis=0)
@@ -414,14 +418,30 @@
             def _():
                 result(slots[1]).start()
 
+            @pl.when(t == 3)
+            def _():
+                own_result().start()
+
+        def step(i, carry):
+            near = jnp.logical_or(i < 3, i == 5)
+
+            @pl.when(near)
+            def _():
+                near_half(jnp.minimum(i, 3))
+
+            @pl.when(i == 3)
+            def _():
+                for kind in range(2):
+                    for d in FAR_FIRST:
+                        forward(kind, column(d), 1 - half).wait_recv()
+
+            @pl.when(jnp.logical_not(near))
+            def _():
+                far_half(i - 3 - i // 6)
+
             return carry
 
-        lax.fori_loop(0, Z // 2, near_half, 0)
-        for kind in range(2):
-            for d in FAR_FIRST:
-                forward(kind, column(d), 1 - half).wait_recv()
-        lax.fori_loop(0, Z // 2, far_half, 0)
-        own_result().start()
+        lax.fori_loop(0, Z, step, 0)
 
     for d in range(1, GROUP):
         sum_copy(d).wait_send()

time: 39.2 us -> 39.5 us (level)
  the two profiles are of different devices: /device:TPU:1 before, /device:TPU:16 now
where the time goes in v3:
time: 39.5 us; the launch traced here: 39.4 us
  Pallas kernels  38.7 us (98%)
  local copies, waits for them, and re-layouts  0.67 us (2%)
    pallas_call x1, Pallas kernels, local(): pl.pallas_call(kernel, out_shape=pltpu.VMEM((streams, ROWS, ROWS), BF16),...  38.7 us

profile of v3, /device:TPU:16, one launch (start us, length us, event | category | flops | bytes accessed | tf_op | source)
XLA Modules:
  0.0 39.4 jit_solution(11301725283115104719)
XLA Ops:
  0.0 38.7 %attend.1 = bf16[5,128,128]{2,1,0:T(8,128)(2,1)S(1)} custom-call(bf16[5,128,128]{2,1,0:T(8,128)(2,1)} %q_hbm.1, bf16[5,128,128]{2,1,0:T(8,128)(2,1)} %k_hbm.1, bf16[5,128,128]{2,1,0:T(8,128)(2,1)} %v_hbm.1, f32[40,128]{1,0:T(8,128)} %qg_hbm.1, f32[40,128]{1,0:T(8,128)} %kg_hbm.1, s32[5,128]{1,0:T(8,128)} %order_hbm.1, s32[5,16]{1,0:T(8,128)} %rows_hbm.1, ...), custom_call_target="tpu_custom_call" | custom-call | tf_op jit(solution)/shard_map/attend/pallas_call | solution.py:469
  38.7 0.7 %copy.10 = bf16[5,128,128]{2,1,0:T(8,128)(2,1)} copy(bf16[5,128,128]{2,1,0:T(8,128)(2,1)S(1)} %attend.1) | data formatting | bytes 327680

commit v4 on v2

--- a/solution.py
+++ b/solution.py
@@ -22,6 +22,7 @@
 MASKED = -(2.0**30)
 FAR_FIRST = (4, 3, 5, 2, 6, 1, 7, 0)
 KEY_CHUNK = 512
+V_FIRST = 2
 PER = KEY_CHUNK // ROWS
 PARTS = Z // PER
 
@@ -35,8 +36,8 @@
 
 def kernel(
     q_hbm, k_hbm, v_hbm, qg_hbm, kg_hbm, order_hbm, rows_hbm, map_hbm, out_ref,
-    qg_ref, kg_ref, order_ref, rows_ref, map_ref, qraw, kraw, qn, kn, sum_out, sum_in, ord_out, ord_in, kbuf, vbuf, qbuf, obuf,
-    oht, mbuf, lbuf, peaks, denoms, mixes, s_scr, bt_scr, a_scr,
+    qg_ref, kg_ref, rows_ref, map_ref, qraw, kraw, qn, kn, sum_out, sum_in, ord_in, kbuf, vbuf, qbuf, obuf,
+    oht, mbuf, lbuf, peaks, denoms, mixes, s_scr, s_two, bt_scr, a_scr,
     raw_sem, sum_send, sum_recv, ord_send, ord_recv, kv_send, kv_recv, fwd_send, fwd_recv,
     ofw_send, ofw_recv, out_send, out_recv,
 ):
@@ -72,7 +73,6 @@
         pltpu.make_async_copy(src, dst, raw_sem.at[2 + i])
         for i, (src, dst) in enumerate(
             (
-                (order_hbm, order_ref),
                 (kg_hbm, kg_ref),
                 (qg_hbm, qg_ref),
                 (rows_hbm, rows_ref),
@@ -80,10 +80,9 @@
             )
         )
     ]
-    small[0].start()
     q_in.start()
     k_in.start()
-    for copy in small[1:]:
+    for copy in small:
         copy.start()
     pl.semaphore_wait(barrier, 2 * (Z - 1) + 1)
 
@@ -141,9 +140,8 @@
 
     def order_piece(d):
         to = column(d)
-        stream, _ = owner_of(to, shift, core)
-        return pltpu.make_async_remote_copy(
-            src_ref=ord_out.at[stream],
+        return pltpu.make_async_remote_copy(
+            src_ref=order_hbm,
             dst_ref=ord_in.at[half, z],
             send_sem=ord_send.at[d],
             recv_sem=ord_recv.at[z],
@@ -152,7 +150,7 @@
         )
 
     def own_order():
-        return pltpu.make_async_copy(ord_out.at[mine], ord_in.at[half, z], ord_recv.at[z])
+        return pltpu.make_async_copy(order_hbm, ord_in.at[half, z], ord_recv.at[z])
 
     def order_arrival(d):
         slot = column(d)
@@ -176,6 +174,16 @@
             device_id_type=MESH,
         )
 
+    def own_value():
+        return pltpu.make_async_remote_copy(
+            src_ref=v_hbm.at[mine],
+            dst_ref=vbuf.at[me],
+            send_sem=fwd_send.at[0, z],
+            recv_sem=fwd_recv.at[0, z],
+            device_id=partner,
+            device_id_type=MESH,
+        )
+
     def order_forward(side):
         return pltpu.make_async_remote_copy(
             src_ref=ord_in.at[side],
@@ -194,11 +202,14 @@
             def _(d=d):
                 make(d)
 
+    to_all(lambda d: order_piece(d).start())
     to_all(lambda d: piece(0, d).start())
-    small[0].wait()
-    sum_out[...] = jnp.zeros((8, ROWS), F32)
-    for j in range(STREAMS):
-        ord_out[j] = jnp.broadcast_to(order_ref[pl.ds(j, 1), :], (8, ROWS))
+
+    @pl.when(busy)
+    def _():
+        own_value().start()
+        own_order().start()
+        own_piece(0).start()
 
     def squares(raw):
         total = jnp.zeros((ROWS, ROWS), F32)
@@ -206,20 +217,15 @@
             x = raw[j].astype(F32)
             total = total + x * x
         return jnp.sum(total.T, axis=0, keepdims=True)
-    to_all(lambda d: order_piece(d).start())
-
-    @pl.when(busy)
-    def _():
-        own_order().start()
-        own_piece(0).start()
-
+
+    sum_out[...] = jnp.zeros((8, ROWS), F32)
     q_in.wait()
     sum_out[pl.ds(0, 1), :] = squares(qraw)
     k_in.wait()
     sum_out[pl.ds(1, 1), :] = squares(kraw)
     for d in range(1, GROUP):
         sum_copy(d).start()
-    for copy in small[1:]:
+    for copy in small:
         copy.wait()
     total = sum_out[...]
     for d in range(1, GROUP):
@@ -237,19 +243,25 @@
         gain = gains[pl.ds(member * STREAMS + stream, 1), :]
         out[stream] = (raw[stream].astype(F32) * rows * gain).astype(BF16)
 
-    for kind in (1, 2):
-        rows = by_row(2 - kind)
-
-        def ready(d, kind=kind, rows=rows):
-            normalize(kind, d, rows)
-            piece(kind, d).start()
-
-        to_all(ready)
-
-        @pl.when(busy)
-        def _(kind=kind, rows=rows):
-            normalize(kind, 0, rows)
-            own_piece(kind).start()
+    rows = by_row(1)
+
+    def ready_key(d):
+        normalize(1, d, rows)
+        piece(1, d).start()
+
+    to_all(ready_key)
+
+    @pl.when(busy)
+    def _():
+        normalize(1, 0, rows)
+        own_piece(1).start()
+
+    rows_q = by_row(0)
+
+    @pl.when(jnp.logical_not(busy))
+    def _():
+        to_all(lambda d: normalize(2, d, rows_q))
+        to_all(lambda d: piece(2, d).start())
 
     def result(slot):
         return pltpu.make_async_remote_copy(
@@ -277,23 +289,33 @@
 
     @pl.when(busy)
     def _():
-        own_piece(0).wait()
-        forward(0, z, half).start()
-        for d in FAR_FIRST[:-1]:
+        for d in FAR_FIRST[:V_FIRST]:
             arrival(0, d).wait_recv()
             forward(0, column(d), half).start()
+
+        def ready_query(d):
+            normalize(2, d, rows_q)
+            piece(2, d).start()
+
+        to_all(ready_query)
+        normalize(2, 0, rows_q)
+        own_piece(2).start()
         own_order().wait()
         for d in FAR_FIRST[:-1]:
             order_arrival(d).wait_recv()
         order_forward(half).start()
+        for d in FAR_FIRST[V_FIRST:-1]:
+            arrival(0, d).wait_recv()
+            forward(0, column(d), half).start()
+        own_piece(0).wait()
         own_piece(1).wait()
         forward(1, z, half).start()
-        for d in FAR_FIRST[:-1]:
+        for d in FAR_FIRST[:4]:
             arrival(1, d).wait_recv()
             forward(1, column(d), half).start()
 
         order_forward(1 - half).wait_recv()
-        tokens = ord_in[:, :, 0, :].reshape(CLUSTERS, ROWS)
+        tokens = ord_in[:, :, pl.ds(mine, 1), :].reshape(CLUSTERS, ROWS)
         place = lax.broadcasted_iota(jnp.int32, (CLUSTERS, ROWS), 0) * ROWS
         place = place + lax.broadcasted_iota(jnp.int32, (CLUSTERS, ROWS), 1)
         owner = jnp.full((CLUSTERS, ROWS), -1, jnp.int32)
@@ -337,48 +359,51 @@
         open_ = jnp.logical_or(map_ref[mine] == 1, same)
         mbuf[pl.ds(0, BLOCKS), pl.ds(0, BLOCKS)] = jnp.where(open_, 0.0, MASKED).astype(BF16)
 
+        for d in FAR_FIRST[4:-1]:
+            arrival(1, d).wait_recv()
+            forward(1, column(d), half).start()
+
         factor = math.log2(math.e) / math.sqrt(ROWS)
 
-        def weigh(left, side, start):
+        def score(left, side, start, into):
             peak = start
             for i in range(PARTS):
                 span = pl.ds(side * Z + i * PER, PER)
+                keys = kbuf[span].reshape(KEY_CHUNK, ROWS)
+                tags = oht[span].reshape(KEY_CHUNK, ROWS)
                 scores = lax.dot_general(
                     left,
-                    jnp.concatenate(
-                        [
-                            kbuf[span].reshape(KEY_CHUNK, ROWS),
-                            oht[span].reshape(KEY_CHUNK, ROWS),
-                        ],
-                        axis=1,
-                    ),
+                    jnp.concatenate([keys, tags], axis=1),
                     (((1,), (1,)), ((), ())),
                     preferred_element_type=F32,
                 )
-                s_scr[:, pl.ds(i * KEY_CHUNK, KEY_CHUNK)] = scores
+                into[:, pl.ds(i * KEY_CHUNK, KEY_CHUNK)] = scores
                 peak = jnp.maximum(peak, jnp.max(scores, axis=1, keepdims=True))
+            return peak
+
+        def mix(peak, side, held):
             denom = jnp.zeros((2 * ROWS, 1), F32)
             mixed = jnp.zeros((2 * ROWS, ROWS), F32)
             for i in range(PARTS):
                 span = pl.ds(side * Z + i * PER, PER)
-                p = jnp.exp2((s_scr[:, pl.ds(i * KEY_CHUNK, KEY_CHUNK)] - peak) * factor)
+                p = jnp.exp2((held[:, pl.ds(i * KEY_CHUNK, KEY_CHUNK)] - peak) * factor)
                 denom = denom + jnp.sum(p, axis=1, keepdims=True)
                 values = vbuf[span].reshape(KEY_CHUNK, ROWS)
                 mixed = mixed + jnp.dot(p.astype(BF16), values, preferred_element_type=F32)
-            return peak, denom, mixed
+            return denom, mixed
 
         def near_half(t, carry):
-            first, second = lax.rem(4 - t, 4), 4 + t
-
-            @pl.when(t == 0)
+            first, second = 4 + t, 3 - t
+            arrival(2, first).wait_recv()
+
+            @pl.when(t < 3)
+            def _():
+                arrival(2, second).wait_recv()
+
+            @pl.when(t == 3)
             def _():
                 own_piece(2).wait()
 
-            @pl.when(t > 0)
-            def _():
-                arrival(2, first).wait_recv()
-
-            arrival(2, second).wait_recv()
             lefts = []
             for d in (first, second):
                 slot = column(d)
@@ -386,9 +411,9 @@
                 left = jnp.concatenate([qbuf[slot], bias.astype(BF16)], axis=1)
                 lbuf[slot] = left
                 lefts.append(left)
-            peak, denom, mixed = weigh(
-                jnp.concatenate(lefts, axis=0), half, jnp.full((2 * ROWS, 1), -jnp.inf, F32)
-            )
+            start = jnp.full((2 * ROWS, 1), -jnp.inf, F32)
+            peak = score(jnp.concatenate(lefts, axis=0), half, start, s_scr)
+            denom, mixed = mix(peak, half, s_scr)
             for i, d in enumerate((first, second)):
                 slot = column(d)
                 rows = slice(i * ROWS, (i + 1) * ROWS)
@@ -397,30 +422,35 @@
                 mixes[slot] = mixed[rows]
             return carry
 
-        def far_half(t, carry):
+        lax.fori_loop(0, Z // 2, near_half, 0)
+        for kind in range(2):
+            for d in FAR_FIRST:
+                forward(kind, column(d), 1 - half).wait_recv()
+
+        def far_score(t):
             slots = (column(4 + t), column(3 - t))
             left = jnp.concatenate([lbuf[slot] for slot in slots], axis=0)
             before = jnp.concatenate([peaks[slot] for slot in slots], axis=0)
-            peak, denom, mixed = weigh(left, 1 - half, before)
+            return before, score(left, 1 - half, before, (s_scr, s_two)[t % 2])
+
+        def far_mix(t, before, peak):
+            slots = (column(4 + t), column(3 - t))
+            denom, mixed = mix(peak, 1 - half, (s_scr, s_two)[t % 2])
             fade = jnp.exp2((before - peak) * factor)
             denom = denom + fade * jnp.concatenate([denoms[slot] for slot in slots], axis=0)
             mixed = mixed + fade * jnp.concatenate([mixes[slot] for slot in slots], axis=0)
             out = (mixed / denom).astype(BF16)
             for i, slot in enumerate(slots):
                 obuf[slot] = out[i * ROWS : (i + 1) * ROWS]
-            result(slots[0]).start()
-
-            @pl.when(t < 3)
-            def _():
-                result(slots[1]).start()
-
-            return carry
-
-        lax.fori_loop(0, Z // 2, near_half, 0)
-        for kind in range(2):
-            for d in FAR_FIRST:
-                forward(kind, column(d), 1 - half).wait_recv()
-        lax.fori_loop(0, Z // 2, far_half, 0)
+
+        held = far_score(0)
+        for t in range(Z // 2):
+            ahead = far_score(t + 1) if t < 3 else None
+            far_mix(t, *held)
+            held = ahead
+            result(column(4 + t)).start()
+            if t < 3:
+                result(column(3 - t)).start()
         own_result().start()
 
     for d in range(1, GROUP):
@@ -454,7 +484,6 @@
         scratch_shapes=[
             pltpu.VMEM((HEADS, ROWS), F32),
             pltpu.VMEM((HEADS, ROWS), F32),
-            pltpu.VMEM((STREAMS, ROWS), jnp.int32),
             pltpu.SMEM((STREAMS, CLUSTERS), jnp.int32),
             pltpu.VMEM((STREAMS, BLOCKS, BLOCKS), jnp.int32),
             pltpu.VMEM((STREAMS, ROWS, ROWS), BF16),
@@ -463,8 +492,7 @@
             pltpu.VMEM((STREAMS, ROWS, ROWS), BF16),
             pltpu.VMEM((8, ROWS), F32),
             pltpu.VMEM((GROUP, 8, ROWS), F32),
-            pltpu.VMEM((STREAMS, 8, ROWS), jnp.int32),
-            pltpu.VMEM((2, Z, 8, ROWS), jnp.int32),
+            pltpu.VMEM((2, Z, STREAMS, ROWS), jnp.int32),
             pltpu.VMEM((2 * Z, ROWS, ROWS), BF16),
             pltpu.VMEM((2 * Z, ROWS, ROWS), BF16),
             pltpu.VMEM((Z, ROWS, ROWS), BF16),
@@ -476,9 +504,10 @@
             pltpu.VMEM((Z, ROWS, 1), F32),
             pltpu.VMEM((Z, ROWS, ROWS), F32),
             pltpu.VMEM((2 * ROWS, Z * ROWS), F32),
+            pltpu.VMEM((2 * ROWS, Z * ROWS), F32),
             pltpu.VMEM((ROWS, 2 * Z * ROWS), BF16),
             pltpu.VMEM((CLUSTERS, 2 * Z * ROWS), BF16),
-            sems((7,)),
+            sems((6,)),
             sems((GROUP - 1,)),
             sems((GROUP,)),
             sems((Z,)),

time: 39.2 us -> 38.3 us (0.977)
  Pallas kernels: 38.3 us -> 37.3 us
    pallas_call x1, Pallas kernels: 38.3 us -> 37.3 us  [local(): pl.pallas_call(kernel, out_shape=pltpu.VMEM((streams, ROWS, ROWS), BF16),...]
where the time goes in v4:
time: 38.3 us; the launch traced here: 38 us
  Pallas kernels  37.3 us (97%)
  local copies, waits for them, and re-layouts  0.67 us (2%)
    pallas_call x1, Pallas kernels, local(): pl.pallas_call(kernel, out_shape=pltpu.VMEM((streams, ROWS, ROWS), BF16),...  37.3 us

profile of v4, /device:TPU:1, one launch (start us, length us, event | category | flops | bytes accessed | tf_op | source)
XLA Modules:
  0.0 38.0 jit_solution(1738013764582912003)
XLA Ops:
  0.0 37.3 %attend.1 = bf16[5,128,128]{2,1,0:T(8,128)(2,1)S(1)} custom-call(bf16[5,128,128]{2,1,0:T(8,128)(2,1)} %q_hbm.1, bf16[5,128,128]{2,1,0:T(8,128)(2,1)} %k_hbm.1, bf16[5,128,128]{2,1,0:T(8,128)(2,1)} %v_hbm.1, f32[40,128]{1,0:T(8,128)} %qg_hbm.1, f32[40,128]{1,0:T(8,128)} %kg_hbm.1, s32[5,128]{1,0:T(8,128)} %order_hbm.1, s32[5,16]{1,0:T(8,128)} %rows_hbm.1, ...), custom_call_target="tpu_custom_call" | custom-call | tf_op jit(solution)/shard_map/attend/pallas_call | solution.py:479
  37.3 0.7 %copy.10 = bf16[5,128,128]{2,1,0:T(8,128)(2,1)} copy(bf16[5,128,128]{2,1,0:T(8,128)(2,1)S(1)} %attend.1) | data formatting | bytes 327680

commit v5 on v4

--- a/solution.py
+++ b/solution.py
@@ -34,11 +34,15 @@
     return stream, busy
 
 
+def pair_of(d):
+    return d - 4 if d >= 4 else 3 - d
+
+
 def kernel(
     q_hbm, k_hbm, v_hbm, qg_hbm, kg_hbm, order_hbm, rows_hbm, map_hbm, out_ref,
     qg_ref, kg_ref, rows_ref, map_ref, qraw, kraw, qn, kn, sum_out, sum_in, ord_in, kbuf, vbuf, qbuf, obuf,
     oht, mbuf, lbuf, peaks, denoms, mixes, s_scr, s_two, bt_scr, a_scr,
-    raw_sem, sum_send, sum_recv, ord_send, ord_recv, kv_send, kv_recv, fwd_send, fwd_recv,
+    raw_sem, own_sem, sum_send, sum_recv, ord_send, ord_recv, kv_send, kv_recv, q_recv, fwd_send, fwd_recv,
     ofw_send, ofw_recv, out_send, out_recv,
 ):
     me = lax.axis_index("seq")
@@ -90,22 +94,23 @@
         return pltpu.make_async_remote_copy(
             src_ref=sum_out,
             dst_ref=sum_in.at[member],
-            send_sem=sum_send.at[d - 1],
-            recv_sem=sum_recv.at[member],
+            send_sem=sum_send.at[0],
+            recv_sem=sum_recv.at[0],
             device_id={"head": video + lax.rem(member + d, GROUP)},
             device_id_type=MESH,
         )
 
-    def sum_arrival(d):
-        slot = lax.rem(member + d, GROUP)
-        return pltpu.make_async_remote_copy(
-            src_ref=sum_out,
-            dst_ref=sum_in.at[slot],
-            send_sem=sum_send.at[d - 1],
-            recv_sem=sum_recv.at[slot],
-            device_id={"head": video + slot},
-            device_id_type=MESH,
-        )
+    def waiting(ref, send_sem, recv_sem):
+        return pltpu.make_async_remote_copy(
+            src_ref=ref,
+            dst_ref=ref,
+            send_sem=send_sem,
+            recv_sem=recv_sem,
+            device_id=partner,
+            device_id_type=MESH,
+        )
+
+    all_sums = waiting(sum_in.at[pl.ds(0, GROUP - 1)], sum_send.at[0], sum_recv.at[0])
 
     def piece(kind, d):
         to = column(d)
@@ -115,8 +120,8 @@
         return pltpu.make_async_remote_copy(
             src_ref=src,
             dst_ref=dst,
-            send_sem=kv_send.at[kind, d],
-            recv_sem=kv_recv.at[kind, z],
+            send_sem=kv_send.at[0],
+            recv_sem=q_recv.at[pair_of(Z - d)] if kind == 2 else kv_recv.at[kind, z],
             device_id={"seq": half * Z + to},
             device_id_type=MESH,
         )
@@ -124,52 +129,34 @@
     def own_piece(kind):
         src = (v_hbm, kn, qn)[kind].at[mine]
         dst = (vbuf.at[me], kbuf.at[me], qbuf.at[z])[kind]
-        return pltpu.make_async_copy(src, dst, kv_recv.at[kind, z])
+        return pltpu.make_async_copy(src, dst, own_sem.at[0] if kind == 2 else kv_recv.at[kind, z])
 
     def arrival(kind, d):
         slot = column(d)
-        dst = (vbuf.at[half * Z + slot], kbuf.at[half * Z + slot], qbuf.at[slot])[kind]
-        return pltpu.make_async_remote_copy(
-            src_ref=dst,
-            dst_ref=dst,
-            send_sem=kv_send.at[kind, d],
-            recv_sem=kv_recv.at[kind, slot],
-            device_id={"seq": half * Z + slot},
-            device_id_type=MESH,
-        )
+        buf = (vbuf, kbuf)[kind]
+        return waiting(buf.at[half * Z + slot], kv_send.at[0], kv_recv.at[kind, slot])
 
     def order_piece(d):
         to = column(d)
         return pltpu.make_async_remote_copy(
             src_ref=order_hbm,
             dst_ref=ord_in.at[half, z],
-            send_sem=ord_send.at[d],
-            recv_sem=ord_recv.at[z],
+            send_sem=ord_send.at[0],
+            recv_sem=ord_recv.at[0],
             device_id={"seq": half * Z + to},
             device_id_type=MESH,
         )
 
     def own_order():
-        return pltpu.make_async_copy(order_hbm, ord_in.at[half, z], ord_recv.at[z])
-
-    def order_arrival(d):
-        slot = column(d)
-        return pltpu.make_async_remote_copy(
-            src_ref=ord_in.at[half, slot],
-            dst_ref=ord_in.at[half, slot],
-            send_sem=ord_send.at[d],
-            recv_sem=ord_recv.at[slot],
-            device_id={"seq": half * Z + slot},
-            device_id_type=MESH,
-        )
+        return pltpu.make_async_copy(order_hbm, ord_in.at[half, z], own_sem.at[1])
 
     def forward(kind, slot, side):
         buf = (vbuf, kbuf)[kind]
         return pltpu.make_async_remote_copy(
             src_ref=buf.at[side * Z + slot],
             dst_ref=buf.at[side * Z + slot],
-            send_sem=fwd_send.at[kind, slot],
-            recv_sem=fwd_recv.at[kind, slot],
+            send_sem=fwd_send.at[0],
+            recv_sem=fwd_recv.at[0],
             device_id=partner,
             device_id_type=MESH,
         )
@@ -178,11 +165,13 @@
         return pltpu.make_async_remote_copy(
             src_ref=v_hbm.at[mine],
             dst_ref=vbuf.at[me],
-            send_sem=fwd_send.at[0, z],
-            recv_sem=fwd_recv.at[0, z],
+            send_sem=fwd_send.at[0],
+            recv_sem=fwd_recv.at[0],
             device_id=partner,
             device_id_type=MESH,
         )
+
+    all_forwards = waiting(kbuf, fwd_send.at[0], fwd_recv.at[0])
 
     def order_forward(side):
         return pltpu.make_async_remote_copy(
@@ -228,8 +217,7 @@
     for copy in small:
         copy.wait()
     total = sum_out[...]
-    for d in range(1, GROUP):
-        sum_arrival(d).wait_recv()
+    all_sums.wait_recv()
     for d in range(1, GROUP):
         total = total + sum_in[lax.rem(member + d, GROUP)]
     scale = lax.rsqrt(total * (1.0 / (HEADS * ROWS)) + EPS)
@@ -267,25 +255,14 @@
         return pltpu.make_async_remote_copy(
             src_ref=obuf.at[slot],
             dst_ref=out_ref.at[mine],
-            send_sem=out_send.at[slot],
-            recv_sem=out_recv.at[mine],
+            send_sem=out_send.at[0],
+            recv_sem=out_recv.at[0],
             device_id={"seq": half * Z + slot},
             device_id_type=MESH,
         )
 
     def own_result():
-        return pltpu.make_async_copy(obuf.at[z], out_ref.at[mine], out_recv.at[mine])
-
-    def result_arrival(d):
-        stream, _ = owner_of(column(d), shift, core)
-        return pltpu.make_async_remote_copy(
-            src_ref=obuf.at[0],
-            dst_ref=out_ref.at[stream],
-            send_sem=out_send.at[0],
-            recv_sem=out_recv.at[stream],
-            device_id={"seq": half * Z + column(d)},
-            device_id_type=MESH,
-        )
+        return pltpu.make_async_copy(obuf.at[z], out_ref.at[mine], own_sem.at[2])
 
     @pl.when(busy)
     def _():
@@ -301,8 +278,7 @@
         normalize(2, 0, rows_q)
         own_piece(2).start()
         own_order().wait()
-        for d in FAR_FIRST[:-1]:
-            order_arrival(d).wait_recv()
+        waiting(ord_in.at[half, pl.ds(0, Z - 1)], ord_send.at[0], ord_recv.at[0]).wait_recv()
         order_forward(half).start()
         for d in FAR_FIRST[V_FIRST:-1]:
             arrival(0, d).wait_recv()
@@ -394,14 +370,13 @@
 
         def near_half(t, carry):
             first, second = 4 + t, 3 - t
-            arrival(2, first).wait_recv()
-
             @pl.when(t < 3)
             def _():
-                arrival(2, second).wait_recv()
+                waiting(qbuf.at[pl.ds(0, 2)], kv_send.at[0], q_recv.at[t]).wait_recv()
 
             @pl.when(t == 3)
             def _():
+                waiting(qbuf.at[0], kv_send.at[0], q_recv.at[t]).wait_recv()
                 own_piece(2).wait()
 
             lefts = []
@@ -423,9 +398,7 @@
             return carry
 
         lax.fori_loop(0, Z // 2, near_half, 0)
-        for kind in range(2):
-            for d in FAR_FIRST:
-                forward(kind, column(d), 1 - half).wait_recv()
+        all_forwards.wait_recv()
 
         def far_score(t):
             slots = (column(4 + t), column(3 - t))
@@ -453,23 +426,26 @@
                 result(column(3 - t)).start()
         own_result().start()
 
-    for d in range(1, GROUP):
-        sum_copy(d).wait_send()
-    to_all(lambda d: order_piece(d).wait_send())
-    for kind in range(3):
-        to_all(lambda d, kind=kind: piece(kind, d).wait_send())
-
+    all_sums.wait_send()
     @pl.when(busy)
     def _():
         order_forward(half).wait_send()
-        for kind in range(2):
-            for d in FAR_FIRST:
-                forward(kind, column(d), half).wait_send()
-        for d in FAR_FIRST[:-1]:
-            result(column(d)).wait_send()
+        all_forwards.wait_send()
+        waiting(obuf.at[pl.ds(0, Z - 1)], out_send.at[0], out_recv.at[0]).wait_send()
         own_result().wait()
 
-    to_all(lambda d: result_arrival(d).wait_recv())
+    def settle(streams):
+        waiting(ord_in.at[0, pl.ds(0, streams)], ord_send.at[0], ord_recv.at[0]).wait_send()
+        waiting(kbuf.at[pl.ds(0, 3 * streams)], kv_send.at[0], kv_recv.at[0, 0]).wait_send()
+        waiting(obuf.at[pl.ds(0, streams)], out_send.at[0], out_recv.at[0]).wait_recv()
+
+    @pl.when(busy)
+    def _():
+        settle(STREAMS - 1)
+
+    @pl.when(jnp.logical_not(busy))
+    def _():
+        settle(STREAMS)
 
 
 def local(query, key, value, q_gain, k_gain, order, cluster_rows, block_map):
@@ -480,7 +456,7 @@
         kernel,
         out_shape=pltpu.VMEM((streams, ROWS, ROWS), BF16),
         in_specs=[any_] * 8,
-        out_specs=pl.BlockSpec(memory_space=pltpu.VMEM),
+        out_specs=any_,
         scratch_shapes=[
             pltpu.VMEM((HEADS, ROWS), F32),
             pltpu.VMEM((HEADS, ROWS), F32),
@@ -508,18 +484,20 @@
             pltpu.VMEM((ROWS, 2 * Z * ROWS), BF16),
             pltpu.VMEM((CLUSTERS, 2 * Z * ROWS), BF16),
             sems((6,)),
-            sems((GROUP - 1,)),
-            sems((GROUP,)),
-            sems((Z,)),
-            sems((Z,)),
-            sems((3, Z)),
-            sems((3, Z)),
+            sems((3,)),
+            sems((1,)),
+            sems((1,)),
+            sems((1,)),
+            sems((1,)),
+            sems((1,)),
             sems((2, Z)),
-            sems((2, Z)),
-            sems((1,)),
-            sems((1,)),
-            sems((Z,)),
-            sems((STREAMS,)),
+            sems((4,)),
+            sems((1,)),
+            sems((1,)),
+            sems((1,)),
+            sems((1,)),
+            sems((1,)),
+            sems((1,)),
         ],
         compiler_params=pltpu.CompilerParams(collective_id=0, has_side_effects=True),
         name="attend",

time: 38.3 us -> 37.5 us (0.979)
  Pallas kernels: 37.3 us -> 36.5 us
    pallas_call x1, Pallas kernels: 37.3 us -> 36.5 us  [local(): pl.pallas_call(kernel, out_shape=pltpu.VMEM((streams, ROWS, ROWS), BF16),...]
where the time goes in v5:
time: 37.5 us; the launch traced here: 37.2 us
  Pallas kernels  36.5 us (97%)
  local copies, waits for them, and re-layouts  0.67 us (2%)
    pallas_call x1, Pallas kernels, local(): pl.pallas_call(kernel, out_shape=pltpu.VMEM((streams, ROWS, ROWS), BF16),...  36.5 us

profile of v5, /device:TPU:1, one launch (start us, length us, event | category | flops | bytes accessed | tf_op | source)
XLA Modules:
  0.0 37.2 jit_solution(7057885548167706841)
XLA Ops:
  0.0 36.5 %attend.1 = bf16[5,128,128]{2,1,0:T(8,128)(2,1)S(1)} custom-call(bf16[5,128,128]{2,1,0:T(8,128)(2,1)} %q_hbm.1, bf16[5,128,128]{2,1,0:T(8,128)(2,1)} %k_hbm.1, bf16[5,128,128]{2,1,0:T(8,128)(2,1)} %v_hbm.1, f32[40,128]{1,0:T(8,128)} %qg_hbm.1, f32[40,128]{1,0:T(8,128)} %kg_hbm.1, s32[5,128]{1,0:T(8,128)} %order_hbm.1, s32[5,16]{1,0:T(8,128)} %rows_hbm.1, ...), custom_call_target="tpu_custom_call" | custom-call | tf_op jit(solution)/shard_map/attend/pallas_call | solution.py:455
  36.5 0.7 %copy.10 = bf16[5,128,128]{2,1,0:T(8,128)(2,1)} copy(bf16[5,128,128]{2,1,0:T(8,128)(2,1)S(1)} %attend.1) | data formatting | bytes 327680

commit v6 on v5

--- a/solution.py
+++ b/solution.py
@@ -161,6 +161,16 @@
             device_id_type=MESH,
         )
 
+    def own_key():
+        return pltpu.make_async_remote_copy(
+            src_ref=kn.at[mine],
+            dst_ref=kbuf.at[me],
+            send_sem=fwd_send.at[0],
+            recv_sem=fwd_recv.at[0],
+            device_id=partner,
+            device_id_type=MESH,
+        )
+
     def own_value():
         return pltpu.make_async_remote_copy(
             src_ref=v_hbm.at[mine],
@@ -243,6 +253,7 @@
     def _():
         normalize(1, 0, rows)
         own_piece(1).start()
+        own_key().start()
 
     rows_q = by_row(0)
 
@@ -284,12 +295,6 @@
             arrival(0, d).wait_recv()
             forward(0, column(d), half).start()
         own_piece(0).wait()
-        own_piece(1).wait()
-        forward(1, z, half).start()
-        for d in FAR_FIRST[:4]:
-            arrival(1, d).wait_recv()
-            forward(1, column(d), half).start()
-
         order_forward(1 - half).wait_recv()
         tokens = ord_in[:, :, pl.ds(mine, 1), :].reshape(CLUSTERS, ROWS)
         place = lax.broadcasted_iota(jnp.int32, (CLUSTERS, ROWS), 0) * ROWS
@@ -335,6 +340,10 @@
         open_ = jnp.logical_or(map_ref[mine] == 1, same)
         mbuf[pl.ds(0, BLOCKS), pl.ds(0, BLOCKS)] = jnp.where(open_, 0.0, MASKED).astype(BF16)
 
+        own_piece(1).wait()
+        for d in FAR_FIRST[:4]:
+            arrival(1, d).wait_recv()
+            forward(1, column(d), half).start()
         for d in FAR_FIRST[4:-1]:
             arrival(1, d).wait_recv()
             forward(1, column(d), half).start()

time: 37.5 us -> 37.4 us (level)
  no operation moved by 1% of the time
where the time goes in v6:
time: 37.4 us; the launch traced here: 37.3 us
  Pallas kernels  36.7 us (98%)
  local copies, waits for them, and re-layouts  0.67 us (2%)
    pallas_call x1, Pallas kernels, local(): pl.pallas_call(kernel, out_shape=pltpu.VMEM((streams, ROWS, ROWS), BF16),...  36.7 us

profile of v6, /device:TPU:1, one launch (start us, length us, event | category | flops | bytes accessed | tf_op | source)
XLA Modules:
  0.0 37.3 jit_solution(10445356928535604888)
XLA Ops:
  0.0 36.7 %attend.1 = bf16[5,128,128]{2,1,0:T(8,128)(2,1)S(1)} custom-call(bf16[5,128,128]{2,1,0:T(8,128)(2,1)} %q_hbm.1, bf16[5,128,128]{2,1,0:T(8,128)(2,1)} %k_hbm.1, bf16[5,128,128]{2,1,0:T(8,128)(2,1)} %v_hbm.1, f32[40,128]{1,0:T(8,128)} %qg_hbm.1, f32[40,128]{1,0:T(8,128)} %kg_hbm.1, s32[5,128]{1,0:T(8,128)} %order_hbm.1, s32[5,16]{1,0:T(8,128)} %rows_hbm.1, ...), custom_call_target="tpu_custom_call" | custom-call | tf_op jit(solution)/shard_map/attend/pallas_call | solution.py:464
  36.7 0.7 %copy.10 = bf16[5,128,128]{2,1,0:T(8,128)(2,1)} copy(bf16[5,128,128]{2,1,0:T(8,128)(2,1)S(1)} %attend.1) | data formatting | bytes 327680

commit v7 on v6

--- a/solution.py
+++ b/solution.py
@@ -257,10 +257,14 @@
 
     rows_q = by_row(0)
 
+    def ready_query(d):
+        normalize(2, d, rows_q)
+        piece(2, d).start()
+
+
     @pl.when(jnp.logical_not(busy))
     def _():
-        to_all(lambda d: normalize(2, d, rows_q))
-        to_all(lambda d: piece(2, d).start())
+        to_all(ready_query)
 
     def result(slot):
         return pltpu.make_async_remote_copy(
@@ -280,10 +284,6 @@
         for d in FAR_FIRST[:V_FIRST]:
             arrival(0, d).wait_recv()
             forward(0, column(d), half).start()
-
-        def ready_query(d):
-            normalize(2, d, rows_q)
-            piece(2, d).start()
 
         to_all(ready_query)
         normalize(2, 0, rows_q)

time: 37.4 us -> 37.4 us (level)
  no operation moved by 1% of the time
where the time goes in v7:
time: 37.4 us; the launch traced here: 37.3 us
  Pallas kernels  36.7 us (98%)
  local copies, waits for them, and re-layouts  0.67 us (2%)
    pallas_call x1, Pallas kernels, local(): pl.pallas_call(kernel, out_shape=pltpu.VMEM((streams, ROWS, ROWS), BF16),...  36.7 us

profile of v7, /device:TPU:1, one launch (start us, length us, event | category | flops | bytes accessed | tf_op | source)
XLA Modules:
  0.0 37.3 jit_solution(1376375382880441567)
XLA Ops:
  0.0 36.7 %attend.1 = bf16[5,128,128]{2,1,0:T(8,128)(2,1)S(1)} custom-call(bf16[5,128,128]{2,1,0:T(8,128)(2,1)} %q_hbm.1, bf16[5,128,128]{2,1,0:T(8,128)(2,1)} %k_hbm.1, bf16[5,128,128]{2,1,0:T(8,128)(2,1)} %v_hbm.1, f32[40,128]{1,0:T(8,128)} %qg_hbm.1, f32[40,128]{1,0:T(8,128)} %kg_hbm.1, s32[5,128]{1,0:T(8,128)} %order_hbm.1, s32[5,16]{1,0:T(8,128)} %rows_hbm.1, ...), custom_call_target="tpu_custom_call" | custom-call | tf_op jit(solution)/shard_map/attend/pallas_call | solution.py:464
  36.7 0.7 %copy.10 = bf16[5,128,128]{2,1,0:T(8,128)(2,1)} copy(bf16[5,128,128]{2,1,0:T(8,128)(2,1)S(1)} %attend.1) | data formatting | bytes 327680
